TPU v7x, 32 devices: a whole 2x2x4 slice. The times are simulated.
32 devices in a mesh: expert: 4 (over z), shard: 8 (over y, x, core).
Axes of the slice: x: 2, y: 2, z: 4, core: 2. Of those that a mesh axis runs over, the one named last changes fastest.
Arguments:
- tokens: bfloat16 [4096, 2048], P(('expert', 'shard')), may hold values from -6 to 6
- attn_gain: bfloat16 [2048], P('shard'), may hold values from 0.5 to 1.5
- qkv_weight: bfloat16 [2048, 3, 2048], P(None, None, 'shard'), may hold values from -0.125 to 0.125
- qkv_bias: bfloat16 [3, 2048], P(None, 'shard'), may hold values from -3 to 3
- out_weight: bfloat16 [2048, 2048], P('shard'), may hold values from -1 to 1
- ffn_gain: bfloat16 [2048], P('shard'), may hold values from 0.5 to 1.5
- router_weight: bfloat16 [2048, 8], P('shard'), may hold values from -0.125 to 0.125
- shared_gate_weight: bfloat16 [2048], P('shard'), may hold values from -0.125 to 0.125
- shared_weights: bfloat16 [3, 2048, 5632], P(None, None, 'shard'), may hold values from -0.125 to 0.125
- expert_gate_up: bfloat16 [2048, 8, 2816], P('shard', 'expert'), may hold values from -0.125 to 0.125
- expert_down: bfloat16 [1408, 8, 2048], P('shard', 'expert'), may hold values from -0.15625 to 0.15625
- routes: int32 [4096, 4], P(('expert', 'shard')), may hold values from 0 to 7, all different within a row
- arrival: int32 [32, 512], P(('expert', 'shard')), may hold values from 0 to 511, each once within a row
- cotangent: bfloat16 [4096, 2048], P(('expert', 'shard')), may hold values from -6 to 6
Outputs:
- output: bfloat16 [4096, 2048], P(('expert', 'shard'))
- tokens_grad: bfloat16 [4096, 2048], P(('expert', 'shard'))
- attn_gain_grad: float32 [2048], P('shard')
- qkv_weight_grad: float32 [2048, 3, 2048], P(None, None, 'shard')
- qkv_bias_grad: float32 [3, 2048], P(None, 'shard')
- out_weight_grad: float32 [2048, 2048], P('shard')
- ffn_gain_grad: float32 [2048], P('shard')
- router_weight_grad: float32 [2048, 8], P('shard')
- shared_gate_weight_grad: float32 [2048], P('shard')
- shared_weights_grad: float32 [3, 2048, 5632], P(None, None, 'shard')
- expert_gate_up_grad: float32 [2048, 8, 2816], P('shard', 'expert')
- expert_down_grad: float32 [1408, 8, 2048], P('shard', 'expert')
Inputs may be any that keep to these rules, and one draw needn't show every extreme that they name: `routes`: each row names 4 different experts. `arrival`: each row is a permutation.
All inputs are finite; a program needn't handle non-finite values.
Results may differ from a plain program's by a relative error of at most 0.018.
The roundings to bfloat16 on the way count: a program that leaves them out, or rounds other values in their place, can miss the bound.
Values may be sent and summed in bfloat16 or wider, within the bound.
No kernel may reach another device: no remote copies, remote signals or barrier semaphores. Data moves between devices by JAX's collectives and lax.ppermute only.
A program may use at most 320 MiB of HBM per device.

v0:
```python
import jax
import jax.numpy as jnp
from jax import lax
from jax.sharding import PartitionSpec as P

HEADS = 16
HEAD_DIM = 128
EXPERT_FF = 1408
TOPK = 4


EPSILON = 1e-06
ROPE_BASE = 1000000.0
MASKED = -1e30
HIGHEST = lax.Precision.HIGHEST


def swish(values):
    return values / (1.0 + jnp.exp(-values))


def swish_slope(values):
    logistic = 1.0 / (1.0 + jnp.exp(-values))
    return logistic * (1.0 + values * (1.0 - logistic))


def softmax_rows(scores):
    top = jnp.max(scores, axis=-1, keepdims=True)
    expo = jnp.exp(scores - top)
    return expo / jnp.sum(expo, axis=-1, keepdims=True)


def rope_tables(positions):
    half = HEAD_DIM // 2
    freq = ROPE_BASE ** (-jnp.arange(half, dtype=jnp.float32) * 2.0 / HEAD_DIM)
    angle_tab = positions.astype(jnp.float32)[:, None] * freq[None, :]
    cosine = jnp.cos(angle_tab)
    sine = jnp.sin(angle_tab)
    return (jnp.concatenate([cosine, cosine], 1), jnp.concatenate([sine, sine], 1))


def rotate(values, cosine, sine):
    half = HEAD_DIM // 2
    turned = jnp.concatenate([-values[..., half:], values[..., :half]], -1)
    return values * cosine[:, None, :] + turned * sine[:, None, :]


def rotate_back(grads, cosine, sine):
    half = HEAD_DIM // 2
    scaled = grads * sine[:, None, :]
    turned = jnp.concatenate([scaled[..., half:], -scaled[..., :half]], -1)
    return grads * cosine[:, None, :] + turned


def visible(query_rows, key_rows, prompt_len, cont_len):
    query_col = query_rows[:, None]
    key_line = key_rows[None, :]
    prompt_key = key_line < prompt_len
    same_cont = (
        (key_line >= prompt_len)
        & (query_col >= prompt_len)
        & ((key_line - prompt_len) // cont_len == (query_col - prompt_len) // cont_len)
    )
    return prompt_key & ((query_col >= prompt_len) | (key_line <= query_col)) | same_cont & (
        key_line <= query_col
    )


def per_device(
    tokens,
    attn_gain,
    qkv_weight,
    qkv_bias,
    out_weight,
    ffn_gain,
    router_weight,
    shared_gate_weight,
    shared_weights,
    expert_gate_up,
    expert_down,
    routes,
    arrival,
    cotangent,
):
    shard_count = lax.axis_size("shard")
    expert_count = lax.axis_size("expert")
    rows_local = tokens.shape[0]
    width = tokens.shape[1]
    group_rows = rows_local * shard_count
    prompt_len = group_rows // 2
    local_experts = expert_gate_up.shape[1]
    experts_all = local_experts * expert_count
    capacity = rows_local * TOPK // experts_all
    n_assign = rows_local * TOPK
    head_local = HEADS // shard_count
    head_cols = head_local * HEAD_DIM
    scale = HEAD_DIM ** (-0.5)
    gain_one, gain_two, w_router, w_zgate, w_egu, w_edown = (
        lax.all_gather(attn_gain, "shard", axis=0, tiled=True),
        lax.all_gather(ffn_gain, "shard", axis=0, tiled=True),
        lax.all_gather(router_weight, "shard", axis=0, tiled=True),
        lax.all_gather(shared_gate_weight, "shard", axis=0, tiled=True),
        lax.all_gather(expert_gate_up, "shard", axis=0, tiled=True),
        lax.all_gather(expert_down, "shard", axis=0, tiled=True),
    )
    x_float = tokens.astype(jnp.float32)
    inv_one = lax.rsqrt(jnp.mean(x_float * x_float, axis=1, keepdims=True) + EPSILON)
    normed_one = x_float * inv_one
    gain_one_f = gain_one.astype(jnp.float32)
    attn_in = (normed_one * gain_one_f).astype(jnp.bfloat16)
    w_cols = qkv_weight.reshape(width, 3 * head_cols)
    bias_cols = qkv_bias.reshape(3 * head_cols)
    attn_all = lax.all_gather(attn_in, "shard", axis=0, tiled=True)
    qkv_heads = jnp.dot(attn_all, w_cols, preferred_element_type=jnp.float32) + bias_cols.astype(
        jnp.float32
    )
    group_line = jnp.arange(group_rows, dtype=jnp.int32)
    group_pos = jnp.where(
        group_line < prompt_len, group_line, prompt_len + (group_line - prompt_len) % rows_local
    )
    cos_group, sin_group = rope_tables(group_pos)
    head_shape = (group_rows, head_local, HEAD_DIM)
    q_heads = rotate(qkv_heads[:, :head_cols].reshape(head_shape), cos_group, sin_group).astype(
        jnp.bfloat16
    )
    k_heads = rotate(
        qkv_heads[:, head_cols : 2 * head_cols].reshape(head_shape), cos_group, sin_group
    ).astype(jnp.bfloat16)
    v_heads = qkv_heads[:, 2 * head_cols :].reshape(head_shape).astype(jnp.bfloat16)
    allowed_group = visible(group_line, group_line, prompt_len, rows_local)
    q_first = jnp.moveaxis(q_heads, 1, 0)
    k_first = jnp.moveaxis(k_heads, 1, 0)
    v_first = jnp.moveaxis(v_heads, 1, 0)

    def group_scores(q_one, k_one):
        scores = jnp.dot(q_one, k_one.T, preferred_element_type=jnp.float32) * scale
        return jnp.where(allowed_group, scores, MASKED)

    def forward_one(operands):
        q_one, k_one, v_one = operands
        scores = group_scores(q_one, k_one)
        top = jnp.max(scores, axis=1, keepdims=True)
        expo = jnp.exp(scores - top)
        total = jnp.sum(expo, axis=1, keepdims=True)
        probs = expo / total
        mixed = jnp.dot(probs.astype(jnp.bfloat16), v_one, preferred_element_type=jnp.float32)
        return (mixed, (top + jnp.log(total))[:, 0])

    head_mixed, head_lse = lax.map(forward_one, (q_first, k_first, v_first))
    context_heads = (
        jnp.moveaxis(head_mixed, 0, 1).reshape(group_rows, head_cols).astype(jnp.bfloat16)
    )
    attn_part = jnp.dot(context_heads, out_weight, preferred_element_type=jnp.float32)
    hidden_state = x_float + lax.psum_scatter(attn_part, "shard", scatter_dimension=0, tiled=True)
    inv_two = lax.rsqrt(jnp.mean(hidden_state * hidden_state, axis=1, keepdims=True) + EPSILON)
    normed_two = hidden_state * inv_two
    gain_two_f = gain_two.astype(jnp.float32)
    ffn_in = (normed_two * gain_two_f).astype(jnp.bfloat16)
    router = softmax_rows(jnp.dot(ffn_in, w_router, preferred_element_type=jnp.float32))
    z_logit = jnp.dot(ffn_in, w_zgate, preferred_element_type=jnp.float32)
    z_gate = 1.0 / (1.0 + jnp.exp(-z_logit))
    d_out = cotangent.astype(jnp.float32)
    d_so = (z_gate[:, None] * d_out).astype(jnp.bfloat16)
    ffn_all, d_so_all = (
        lax.all_gather(ffn_in, "shard", axis=0, tiled=True),
        lax.all_gather(d_so, "shard", axis=0, tiled=True),
    )
    gate_pre = jnp.dot(ffn_all, shared_weights[0], preferred_element_type=jnp.float32)
    up_pre = jnp.dot(ffn_all, shared_weights[1], preferred_element_type=jnp.float32)
    shared_hidden = (swish(gate_pre) * up_pre).astype(jnp.bfloat16)
    out_part = jnp.einsum(
        "tf,df->td", shared_hidden, shared_weights[2], preferred_element_type=jnp.float32
    )
    d_sh = jnp.einsum("td,df->tf", d_so_all, shared_weights[2], preferred_element_type=jnp.float32)
    d_gate_s = (d_sh * up_pre * swish_slope(gate_pre)).astype(jnp.bfloat16)
    d_up_s = (d_sh * swish(gate_pre)).astype(jnp.bfloat16)
    d_ffn_part = jnp.einsum(
        "tf,df->td", d_gate_s, shared_weights[0], preferred_element_type=jnp.float32
    ) + jnp.einsum("tf,df->td", d_up_s, shared_weights[1], preferred_element_type=jnp.float32)
    shared_terms = jnp.stack(
        [
            jnp.einsum("td,tf->df", ffn_all, d_gate_s, preferred_element_type=jnp.float32),
            jnp.einsum("td,tf->df", ffn_all, d_up_s, preferred_element_type=jnp.float32),
            jnp.einsum("td,tf->df", d_so_all, shared_hidden, preferred_element_type=jnp.float32),
        ]
    )
    shared_out, d_ffn_shared = (
        lax.psum_scatter(out_part, "shard", scatter_dimension=0, tiled=True),
        lax.psum_scatter(d_ffn_part, "shard", scatter_dimension=0, tiled=True),
    )
    d_zsum = jnp.sum(d_out * shared_out, axis=1)
    route_flat = routes.reshape(-1)
    priority = arrival.reshape(-1)
    same_expert = route_flat[:, None] == route_flat[None, :]
    earlier = priority[None, :] < priority[:, None]
    ranks = jnp.sum((same_expert & earlier).astype(jnp.int32), axis=1)
    kept = ranks < capacity
    slots = jnp.where(kept, route_flat * capacity + ranks, experts_all * capacity)
    table = (
        jnp.full((experts_all * capacity,), n_assign, jnp.int32)
        .at[slots]
        .set(jnp.arange(n_assign, dtype=jnp.int32), mode="drop")
    )
    ffn_pad = jnp.concatenate([ffn_in, jnp.zeros((1, width), jnp.bfloat16)], 0)
    send_rows = ffn_pad[table // TOPK].reshape(expert_count, local_experts, capacity, width)
    arrived = lax.all_to_all(send_rows, "expert", split_axis=0, concat_axis=2, tiled=True)[0]
    e_both = jnp.einsum("erd,def->erf", arrived, w_egu, preferred_element_type=jnp.float32)
    e_gate = e_both[:, :, :EXPERT_FF]
    e_up = e_both[:, :, EXPERT_FF:]
    e_hidden = (swish(e_gate) * e_up).astype(jnp.bfloat16)
    e_out = jnp.einsum(
        "erf,fed->erd", e_hidden, w_edown, preferred_element_type=jnp.float32
    ).astype(jnp.bfloat16)
    returned = lax.all_to_all(
        e_out[None], "expert", split_axis=2, concat_axis=0, tiled=True
    ).reshape(experts_all * capacity, width)
    returned_pad = jnp.concatenate([returned, jnp.zeros((1, width), jnp.bfloat16)], 0)
    gathered = returned_pad[slots].reshape(rows_local, TOPK, width)
    kept_rows = kept.reshape(rows_local, TOPK).astype(jnp.float32)
    onehot = (routes[:, :, None] == jnp.arange(experts_all, dtype=jnp.int32)[None, None, :]).astype(
        jnp.float32
    )
    weight = jnp.sum(onehot * router[:, None, :], axis=2) * kept_rows
    routed = jnp.sum(weight[:, :, None] * gathered.astype(jnp.float32), axis=1)
    output = (hidden_state + routed + z_gate[:, None] * shared_out).astype(jnp.bfloat16)
    d_weight = jnp.sum(d_out[:, None, :] * gathered.astype(jnp.float32), axis=2)
    d_eout = (weight[:, :, None] * d_out[:, None, :]).astype(jnp.bfloat16).reshape(n_assign, width)
    d_eout_pad = jnp.concatenate([d_eout, jnp.zeros((1, width), jnp.bfloat16)], 0)
    d_send = d_eout_pad[table].reshape(expert_count, local_experts, capacity, width)
    d_arrived = lax.all_to_all(d_send, "expert", split_axis=0, concat_axis=2, tiled=True)[0]
    d_eh = jnp.einsum("erd,fed->erf", d_arrived, w_edown, preferred_element_type=jnp.float32)
    d_eboth = jnp.concatenate([d_eh * e_up * swish_slope(e_gate), d_eh * swish(e_gate)], 2).astype(
        jnp.bfloat16
    )
    d_ein = jnp.einsum("erf,def->erd", d_eboth, w_egu, preferred_element_type=jnp.float32).astype(
        jnp.bfloat16
    )
    grad_egu = jnp.einsum("erd,erf->def", arrived, d_eboth, preferred_element_type=jnp.float32)
    grad_edown = jnp.einsum("erf,erd->fed", e_hidden, d_arrived, preferred_element_type=jnp.float32)
    d_back = lax.all_to_all(d_ein[None], "expert", split_axis=2, concat_axis=0, tiled=True).reshape(
        experts_all * capacity, width
    )
    d_back_pad = jnp.concatenate([d_back, jnp.zeros((1, width), jnp.bfloat16)], 0)
    d_routed_in = jnp.sum(
        d_back_pad[slots].reshape(rows_local, TOPK, width).astype(jnp.float32), axis=1
    )
    d_router = jnp.sum(onehot * (d_weight * kept_rows)[:, :, None], axis=1)
    d_logit = (router * (d_router - jnp.sum(d_router * router, axis=1, keepdims=True))).astype(
        jnp.bfloat16
    )
    grad_router = jnp.einsum("td,te->de", ffn_in, d_logit, preferred_element_type=jnp.float32)
    d_zlogit = d_zsum * z_gate * (1.0 - z_gate)
    grad_zgate = jnp.dot(d_zlogit, ffn_in.astype(jnp.float32), precision=HIGHEST)
    d_ffn = (
        d_ffn_shared
        + d_routed_in
        + jnp.einsum("te,de->td", d_logit, w_router, preferred_element_type=jnp.float32)
        + d_zlogit[:, None] * w_zgate.astype(jnp.float32)[None, :]
    )
    grad_gain_two = jnp.sum(d_ffn * normed_two, axis=0)
    d_norm_two = d_ffn * gain_two_f
    d_hidden = d_out + inv_two * (
        d_norm_two - normed_two * jnp.mean(d_norm_two * normed_two, axis=1, keepdims=True)
    )
    d_attn_out = d_hidden.astype(jnp.bfloat16)
    d_ao_all = lax.all_gather(d_attn_out, "shard", axis=0, tiled=True)
    grad_out = jnp.einsum("tc,td->cd", context_heads, d_ao_all, preferred_element_type=jnp.float32)
    d_ctx_heads = jnp.einsum(
        "td,cd->tc", d_ao_all, out_weight, preferred_element_type=jnp.float32
    ).astype(jnp.bfloat16)
    o_first = jnp.moveaxis(d_ctx_heads.reshape(head_shape), 1, 0)

    def backward_one(operands):
        q_one, k_one, v_one, o_one, lse_one = operands
        probs = jnp.exp(group_scores(q_one, k_one) - lse_one[:, None])
        d_probs = jnp.dot(o_one, v_one.T, preferred_element_type=jnp.float32)
        delta = jnp.sum(d_probs * probs, axis=1, keepdims=True)
        d_scores = (probs * (d_probs - delta)).astype(jnp.bfloat16)
        d_query = jnp.dot(d_scores, k_one, preferred_element_type=jnp.float32) * scale
        d_key = jnp.einsum("qk,qd->kd", d_scores, q_one, preferred_element_type=jnp.float32) * scale
        d_value = jnp.einsum(
            "qk,qd->kd", probs.astype(jnp.bfloat16), o_one, preferred_element_type=jnp.float32
        )
        return (d_query, d_key, d_value)

    dq_heads, dk_heads, dv_heads = lax.map(
        backward_one, (q_first, k_first, v_first, o_first, head_lse)
    )
    d_q_pre = rotate_back(jnp.moveaxis(dq_heads, 0, 1), cos_group, sin_group).reshape(
        group_rows, head_cols
    )
    d_k_pre = rotate_back(jnp.moveaxis(dk_heads, 0, 1), cos_group, sin_group).reshape(
        group_rows, head_cols
    )
    d_v_pre = jnp.moveaxis(dv_heads, 0, 1).reshape(group_rows, head_cols)
    d_qkv_heads = jnp.concatenate([d_q_pre, d_k_pre, d_v_pre], 1).astype(jnp.bfloat16)
    grad_bias = jnp.sum(d_qkv_heads.astype(jnp.float32), axis=0).reshape(3, head_cols)
    grad_qkv = jnp.einsum(
        "tc,tf->cf", attn_all, d_qkv_heads, preferred_element_type=jnp.float32
    ).reshape(width, 3, head_cols)
    d_in_part = jnp.einsum("tf,cf->tc", d_qkv_heads, w_cols, preferred_element_type=jnp.float32)
    d_attn_in = lax.psum_scatter(d_in_part, "shard", scatter_dimension=0, tiled=True)
    grad_gain_one = jnp.sum(d_attn_in * normed_one, axis=0)
    d_norm_one = d_attn_in * gain_one_f
    tokens_grad = (
        d_hidden
        + inv_one
        * (d_norm_one - normed_one * jnp.mean(d_norm_one * normed_one, axis=1, keepdims=True))
    ).astype(jnp.bfloat16)
    g_gain_one, g_gain_two, g_router, g_zgate, g_egu, g_edown = (
        lax.psum_scatter(grad_gain_one, "shard", scatter_dimension=0, tiled=True),
        lax.psum_scatter(grad_gain_two, "shard", scatter_dimension=0, tiled=True),
        lax.psum_scatter(grad_router, "shard", scatter_dimension=0, tiled=True),
        lax.psum_scatter(grad_zgate, "shard", scatter_dimension=0, tiled=True),
        lax.psum_scatter(grad_egu, "shard", scatter_dimension=0, tiled=True),
        lax.psum_scatter(grad_edown, "shard", scatter_dimension=0, tiled=True),
    )
    g_gain_one, g_qkv, g_bias, g_out, g_gain_two, g_router, g_zgate, g_shared = lax.psum(
        (g_gain_one, grad_qkv, grad_bias, grad_out, g_gain_two, g_router, g_zgate, shared_terms),
        "expert",
    )
    return (
        output,
        tokens_grad,
        g_gain_one,
        g_qkv,
        g_bias,
        g_out,
        g_gain_two,
        g_router,
        g_zgate,
        g_shared,
        g_egu,
        g_edown,
    )


def solution(mesh):
    placed = (
        P(("expert", "shard"), None),
        P("shard"),
        P(None, None, "shard"),
        P(None, "shard"),
        P("shard", None),
        P("shard"),
        P("shard", None),
        P("shard"),
        P(None, None, "shard"),
        P("shard", "expert", None),
        P("shard", "expert", None),
        P(("expert", "shard"), None),
        P(("expert", "shard"), None),
        P(("expert", "shard"), None),
    )
    return jax.shard_map(
        per_device,
        mesh=mesh,
        in_specs=placed,
        out_specs=(
            P(("expert", "shard"), None),
            P(("expert", "shard"), None),
            P("shard"),
            P(None, None, "shard"),
            P(None, "shard"),
            P("shard", None),
            P("shard"),
            P("shard", None),
            P("shard"),
            P(None, None, "shard"),
            P("shard", "expert", None),
            P("shard", "expert", None),
        ),
        check_vma=False,
    )
```

profile of v0, /device:TPU:0, one launch (start us, length us, event | category | flops | bytes accessed | tf_op | source)
XLA Modules:
  0.0 2185.1 jit_solution(8331764347845348276)
XLA Ops:
  8.0 10.3 all-gather
  22.2 4.7 copy.149
  31.9 27.4 %all-gather.10.cloned.1.call-done = bf16[1024,2048]{1,0:T(8,128)(2,1)} async-done(((bf16[128,2048]{1,0:T(8,128)(2,1)}), bf16[1024,2048]{1,0:T(8,128)(2,1)}) %all-gather.10.cloned.1.call-update) | async-done | bytes 4194320 | tf_op jit(solution)/shard_map/all_gather | solution.py:113
  59.3 6.2 convolution_add_fusion.2
  74.3 13.2 while.28
  74.3 3.7 fusion.193
  80.9 3.7 fusion.193
  87.5 5.7 fusion.130
  93.9 8.8 all-gather.1
  102.8 61.9 %reduce-scatter.7.cloned.1.call-done = f32[128,2048]{1,0:T(8,128)} async-done(((f32[1024,2048]{1,0:T(8,128)}), f32[128,2048]{1,0:T(8,128)}) %reduce-scatter.7.cloned.1.call-update) | async-done | bytes 1048592 | tf_op jit(solution)/shard_map/reduce_scatter | solution.py:154
  168.2 8.8 all-gather.2
  179.3 3.6 copy.165
  186.4 18.6 all-gather.16.cloned.1.call-done
  205.0 8.0 fusion.63
  213.0 6.8 fusion.59
  219.8 24.5 %all-gather.18.cloned.1.call-done = bf16[1024,2048]{1,0:T(8,128)(2,1)} async-done(((bf16[128,2048]{1,0:T(8,128)(2,1)}), bf16[1024,2048]{1,0:T(8,128)(2,1)}) %all-gather.18.cloned.1.call-update) | async-done | bytes 4194320 | tf_op jit(solution)/shard_map/all_gather | solution.py:166
  244.3 10.5 multiply_convert_fusion.4
  255.8 7.9 fusion.56
  271.5 4.6 all-to-all-start
  279.2 5.3 mul.402
  284.5 9.0 all_gather.33
  300.4 24.6 %all-to-all-done = bf16[4,2,64,2048]{3,2,1,0:T(8,128)(2,1)} async-done(((bf16[4,2,64,2048]{3,2,1,0:T(8,128)(2,1)}), bf16[4,2,64,2048]{3,2,1,0:T(8,128)(2,1)}, u32[]{:S(2)}, u32[]{:S(2)}) %all-to-all-start) | async-done | bytes 2097184 | tf_op jit(solution)/shard_map/all_to_all | solution.py:206
  324.9 4.4 all-to-all-start.2
  329.5 5.8 fusion.61
  335.3 7.9 convolution_add_fusion
  344.9 32.4 %all-to-all-done.2 = bf16[4,2,64,2048]{3,2,1,0:T(8,128)(2,1)} async-done(((bf16[4,2,64,2048]{3,2,1,0:T(8,128)(2,1)}), bf16[4,2,64,2048]{3,2,1,0:T(8,128)(2,1)}, u32[]{:S(2)}, u32[]{:S(2)}) %all-to-all-start.2) | async-done | bytes 2097184 | tf_op jit(solution)/shard_map/all_to_all | solution.py:230
  380.5 13.2 fusion.131
  393.7 38.7 %all-gather.14.cloned.1.call-done = bf16[1408,2,2048]{2,0,1:T(8,128)(2,1)} async-done(((bf16[176,2,2048]{2,0,1:T(8,128)(2,1)}), bf16[1408,2,2048]{2,0,1:T(8,128)(2,1)}) %all-gather.14.cloned.1.call-update) | async-done | bytes 11534352 | tf_op jit(solution)/shard_map/all_gather | solution.py:104
  432.4 12.3 multiply_convert_fusion.3
  444.7 11.0 fusion.67
  459.2 4.7 all-to-all-start.1
  463.9 12.2 fusion.68
  479.5 33.1 %all-to-all-done.1 = bf16[1,2,256,2048]{3,1,0,2:T(2,128)(2,1)} async-done(((bf16[1,2,256,2048]{3,1,0,2:T(2,128)(2,1)}), bf16[1,2,256,2048]{3,1,0,2:T(2,128)(2,1)}, u32[]{:S(2)}, u32[]{:S(2)}) %all-to-all-start.1) | async-done | bytes 2097184 | tf_op jit(solution)/shard_map/all_to_all | solution.py:214
  512.7 4.4 all-to-all-start.3
  523.4 3.7 gather_fusion.1
  527.1 4.8 reshape.369
  531.9 6.7 multiply_reduce_fusion.1
  538.7 26.4 %all-to-all-done.3 = bf16[1,2,256,2048]{3,1,0,2:T(2,128)(2,1)} async-done(((bf16[1,2,256,2048]{3,1,0,2:T(2,128)(2,1)}), bf16[1,2,256,2048]{3,1,0,2:T(2,128)(2,1)}, u32[]{:S(2)}, u32[]{:S(2)}) %all-to-all-start.3) | async-done | bytes 2097184 | tf_op jit(solution)/shard_map/all_to_all | solution.py:240
  571.0 4.7 reshape.370
  575.8 6.0 reduce_sum.174
  588.0 13.6 convolution_bitcast_fusion.1
  601.7 34.6 %copy.184 = f32[1408,2,2048]{2,1,0:T(2,128)} copy(f32[1408,2,2048]{0,2,1:T(8,128)} %convolution_bitcast_fusion.1) | data formatting | bytes 46137344 | tf_op jit(solution)/shard_map/erf,erd->fed/transpose | solution.py:239
  642.5 34.8 %while.29 = (s32[]{:T(128)}, f32[2,1024,128]{1,2,0:T(8,128)}, f32[2,1024,128]{1,2,0:T(8,128)}, bf16[2,1024,128]{1,2,0:T(8,128)(2,1)}, bf16[2,1024,128]{2,1,0:T(8...) while((s32[]{:T(128)}, f32[2,1024,128]{1,2,0:T(8,128)}, ...), condition=%wide.region_23.24_spmd.clone, body=%wide.region_21.23_spmd.clone.sunk | while | flops 1360264192 | bytes 66357564 | solution.py:286
  642.6 4.2 subtract_exponential_fusion.4
  659.8 4.2 subtract_exponential_fusion.4
  682.6 5.7 fusion.122
  690.4 21.8 convolution_bitcast_fusion
  712.4 5.7 convolution_bitcast_fusion.2
  724.4 7.5 pad_maximum_fusion
  731.9 6.6 fusion.121
  738.5 6.8 copy.181
  745.3 4.8 fusion.132
  753.4 169.0 %all-reduce.14.cloned.1.call-done = f32[1408,2,2048]{2,1,0:T(2,128)} async-done(((f32[1408,2,2048]{2,1,0:T(2,128)}), f32[1408,2,2048]{2,1,0:T(2,128)}) %all-reduce.14.cloned.1.call-update) | async-done | bytes 23068688
  922.4 4.6 constant_dynamic-slice_fusion.1
  927.0 70.2 %reduce-scatter.13.cloned.1.call-done = f32[128,2048]{1,0:T(8,128)} async-done(((f32[1024,2048]{1,0:T(8,128)}), f32[128,2048]{1,0:T(8,128)}) %reduce-scatter.13.cloned.1.call-update) | async-done | bytes 1048592 | tf_op jit(solution)/shard_map/reduce_scatter | solution.py:302
  998.8 23.5 %all-reduce.8 = (f32[2048]{0:T(1024)S(1)}, f32[2048]{0:T(1024)S(1)}, f32[2048]{0:T(1024)S(1)}) all-reduce(f32[2048]{0:T(1024)S(1)} %get-tuple-element.225, f32[2048]{0:T(1024)S(1)} %copy-done.52, f32[2048]{0:T(1024)S(1)} %bitcast.269), channel_id=6, replica_groups=mesh['expert'=4,'shard'=8] {'shard'}, use_global_device_ids=true, to_apply=%region_27.28.clone | all-reduce | flops 6144 | bytes 49152
  1022.5 11.6 reduce-scatter.15.cloned.1.call-done
  1034.1 19.9 all-reduce.9
  1054.1 4.1 fusion.89
  1058.2 243.9 %reduce-scatter.17.cloned.1.call-done = f32[256,2,2816]{0,2,1:T(8,128)} async-done(((f32[2048,2,2816]{0,2,1:T(8,128)}), f32[256,2,2816]{0,2,1:T(8,128)}) %reduce-scatter.17.cloned.1.call-update) | async-done | bytes 5767184 | tf_op jit(solution)/shard_map/reduce_scatter | solution.py:315
  1302.1 9.6 copy.185
  1311.7 846.8 %all-reduce.16.cloned.1.call-done = (f32[2048,3,256]{2,0,1:T(8,128)}, f32[256,2048]{1,0:T(8,128)}, f32[3,2048,704]{1,2,0:T(8,128)}) async-done(((f32[2048,3,256]{2,0,1:T(8,128)}, f32[256,2048]{1,0:T(8,128)}, f32[3,2048,704]{1,2,0:T(8,128)}), (f32[2048,3,256]{2,0,1:T(8,128)}, f32[256,2048]{1,0:T(8,128)}, f32[3,2048,704]{1,2,0:T(8,128)})) %all-reduce.16.cloned.1.call-update) | async-done | bytes 25690128 | tf_op jit(solution)/shard_map/psum | solution.py:318
  2158.5 6.0 copy.249
  2165.9 12.2 copy.251
  (353 shorter events, 134.1 us)
Async XLA Ops:
  7.2 80.3 %copy-start = (bf16[256,2048]{1,0:T(8,128)(2,1)S(1)}, bf16[256,2048]{1,0:T(8,128)(2,1)}, u32[]{:S(2)}) copy-start(bf16[256,2048]{1,0:T(8,128)(2,1)} %param.22) | copy-start | bytes 3145732
  7.2 52.1 %all-gather.10.cloned.1.call-start = ((), (), s32[]{:S(2)}) async-start(), calls=%async_computation.10 | async-start | bytes 4718592 | tf_op jit(solution)/shard_map/all_gather | solution.py:113
  22.2 142.6 %reduce-scatter.7.cloned.1.call-start = ((), (), s32[]{:S(2)}) async-start(), calls=%async_computation.11 | async-start | bytes 9437184 | tf_op jit(solution)/shard_map/reduce_scatter | solution.py:154
  28.1 37.4 %copy-start.24 = (f32[1024,128]{0,1:T(8,128)}, f32[1024,128]{0,1:T(8,128)S(1)}, u32[]{:S(2)}) copy-start(f32[1024,128]{0,1:T(8,128)S(1)} %get-tuple-element.326) | copy-start | bytes 1572868
  28.1 37.4 %copy-start.30 = (f32[1024,128]{0,1:T(8,128)}, f32[1024,128]{0,1:T(8,128)S(1)}, u32[]{:S(2)}) copy-start(f32[1024,128]{0,1:T(8,128)S(1)} %get-tuple-element.325) | copy-start | bytes 1572868
  87.5 5.8 copy-start.50
  87.5 5.8 copy-start.63
  87.5 5.8 copy-start.70
  87.5 5.8 copy-start.72
  93.3 71.4 %copy-start.16 = (bf16[128,2048]{1,0:T(8,128)(2,1)S(1)}, bf16[128,2048]{1,0:T(8,128)(2,1)}, u32[]{:S(2)}) copy-start(bf16[128,2048]{1,0:T(8,128)(2,1)} %param.18) | copy-start | bytes 1572868
  93.3 74.9 %copy-start.78 = (bf16[256]{0:T(256)(128)(2,1)S(1)}, bf16[256]{0:T(256)(128)(2,1)}, u32[]{:S(2)}) copy-start(bf16[256]{0:T(256)(128)(2,1)} %param.25) | copy-start | bytes 1540
  93.3 84.9 %copy-start.10 = (bf16[128,2048]{1,0:T(8,128)(2,1)S(1)}, bf16[128,2048]{1,0:T(8,128)(2,1)}, u32[]{:S(2)}) copy-start(bf16[128,2048]{1,0:T(8,128)(2,1)} %param.31) | copy-start | bytes 1572868
  93.4 111.7 %all-gather.16.cloned.1.call-start = ((), (), s32[]{:S(2)}) async-start(), calls=%async_computation.14 | async-start | bytes 4718592 | tf_op jit(solution)/shard_map/all_gather | solution.py:165
  102.8 76.5 %copy-start.45 = (f32[8,1,256]{2,1,0:T(1,128)}, f32[8,1,256]{2,1,0:T(1,128)S(1)}, u32[]{:S(2)}) copy-start(f32[8,1,256]{2,1,0:T(1,128)S(1)} %convert_element_type.179) | copy-start | bytes 24580
  166.2 16.8 copy-start.54
  168.2 76.1 %all-gather.18.cloned.1.call-start = ((), (), s32[]{:S(2)}) async-start(), calls=%async_computation.16 | async-start | bytes 4718592 | tf_op jit(solution)/shard_map/all_gather | solution.py:166
  178.3 342.0 %copy-start.60 = (f32[128]{0:T(128)}, f32[128]{0:T(128)S(1)}, u32[]{:S(2)}) copy-start(f32[128]{0:T(128)S(1)} %fusion.83) | copy-start | bytes 1540
  179.3 201.2 %all-gather.12.cloned.1.call-start = ((), (), s32[]{:S(2)}) async-start(), calls=%async_computation.12 | async-start | bytes 25952256 | tf_op jit(solution)/shard_map/all_gather | solution.py:103
  183.0 249.4 %all-gather.14.cloned.1.call-start = ((), (), s32[]{:S(2)}) async-start(), calls=%async_computation.13 | async-start | bytes 12976128 | tf_op jit(solution)/shard_map/all_gather | solution.py:104
  186.4 332.3 %reduce-scatter.9.cloned.1.call-start = ((), (), s32[]{:S(2)}) async-start(), calls=%async_computation.15 | async-start | bytes 9437184 | tf_op jit(solution)/shard_map/reduce_scatter | solution.py:188
  205.0 8.0 copy-start.75
  271.5 53.4 %all-to-all-start = ((bf16[4,2,64,2048]{3,2,1,0:T(8,128)(2,1)}), bf16[4,2,64,2048]{3,2,1,0:T(8,128)(2,1)}, u32[]{:S(2)}, u32[]{:S(2)}) async-start(bf16[4,2,64,2048]{3,2,1,0:T(8,128)(2,1)} %bitcast.236), calls=%async_computation.1 | async-start | bytes 4194304 | tf_op jit(solution)/shard_map/all_to_all | solution.py:206
  279.2 5.3 copy-start.62
  300.4 29.1 %copy-start.82 = (bf16[1024,704]{0,1:T(8,128)(2,1)S(1)}, bf16[1024,704]{0,1:T(8,128)(2,1)}, u32[]{:S(2)}) copy-start(bf16[1024,704]{0,1:T(8,128)(2,1)} %get-tuple-element.296) | copy-start | bytes 4325380
  324.9 52.4 %all-to-all-start.2 = ((bf16[4,2,64,2048]{3,2,1,0:T(8,128)(2,1)}), bf16[4,2,64,2048]{3,2,1,0:T(8,128)(2,1)}, u32[]{:S(2)}, u32[]{:S(2)}) async-start(bf16[4,2,64,2048]{3,2,1,0:T(8,128)(2,1)} %bitcast.237), calls=%async_computation.5 | async-start | bytes 4194304 | tf_op jit(solution)/shard_map/all_to_all | solution.py:230
  329.4 253.6 %reduce-scatter.11.cloned.1.call-start = ((), (), s32[]{:S(2)}) async-start(), calls=%async_computation.17 | async-start | bytes 9437184 | tf_op jit(solution)/shard_map/reduce_scatter | solution.py:189
  329.4 5.8 copy-start.80
  344.9 48.8 %copy-start.3 = (bf16[1,2,4,64,2048]{4,3,2,1,0:T(8,128)(2,1)}, bf16[1,2,4,64,2048]{4,3,2,1,0:T(8,128)(2,1)S(1)}, u32[]{:S(2)}) copy-start(bf16[1,2,4,64,2048]{4,3,2,1,0:T(8,128)(2,1)S(1)} %copy.164) | copy-start | bytes 6291460
  444.7 11.0 copy-start.44
  459.2 53.5 %all-to-all-start.1 = ((bf16[1,2,256,2048]{3,1,0,2:T(2,128)(2,1)}), bf16[1,2,256,2048]{3,1,0,2:T(2,128)(2,1)}, u32[]{:S(2)}, u32[]{:S(2)}) async-start(bf16[1,2,256,2048]{3,1,0,2:T(2,128)(2,1)} %copy.167), calls=%async_computation.2 | async-start | bytes 4194304 | tf_op jit(solution)/shard_map/all_to_all | solution.py:214
  479.5 37.6 %copy-start.11 = (bf16[128,2048]{1,0:T(8,128)(2,1)S(1)}, bf16[128,2048]{1,0:T(8,128)(2,1)}, u32[]{:S(2)}) copy-start(bf16[128,2048]{1,0:T(8,128)(2,1)} %param.31) | copy-start | bytes 1572868
  512.7 52.4 %all-to-all-start.3 = ((bf16[1,2,256,2048]{3,1,0,2:T(2,128)(2,1)}), bf16[1,2,256,2048]{3,1,0,2:T(2,128)(2,1)}, u32[]{:S(2)}, u32[]{:S(2)}) async-start(bf16[1,2,256,2048]{3,1,0,2:T(2,128)(2,1)} %copy.171), calls=%async_computation.6 | async-start | bytes 4194304 | tf_op jit(solution)/shard_map/all_to_all | solution.py:240
  517.1 119.4 %all-gather.20.cloned.1.call-start = ((), (), s32[]{:S(2)}) async-start(), calls=%async_computation.18 | async-start | bytes 4718592 | tf_op jit(solution)/shard_map/all_gather | solution.py:266
  520.3 62.6 %copy-start.67 = (f32[128]{0:T(128)}, f32[128]{0:T(128)S(1)}, u32[]{:S(2)}) copy-start(f32[128]{0:T(128)S(1)} %subtract_multiply_fusion) | copy-start | bytes 1540
  575.8 7.2 copy-start.6
  575.8 7.2 copy-start.46
  575.8 7.2 copy-start.55
  581.7 5.1 copy-start.12
  585.8 15.9 copy-start.65
  588.0 334.4 %all-reduce.14.cloned.1.call-start = ((), (), s32[]{:S(2)}) async-start(), calls=%async_computation.22 | async-start | bytes 46137344
  636.3 360.9 %reduce-scatter.13.cloned.1.call-start = ((), (), s32[]{:S(2)}) async-start(), calls=%async_computation.19 | async-start | bytes 9437184 | tf_op jit(solution)/shard_map/reduce_scatter | solution.py:302
  688.3 345.8 %reduce-scatter.15.cloned.1.call-start = ((), (), s32[]{:S(2)}) async-start(), calls=%async_computation.20 | async-start | bytes 73728 | tf_op jit(solution)/shard_map/reduce_scatter | solution.py:313
  690.2 611.9 %reduce-scatter.17.cloned.1.call-start = ((), (), s32[]{:S(2)}) async-start(), calls=%async_computation.21 | async-start | bytes 51904512 | tf_op jit(solution)/shard_map/reduce_scatter | solution.py:315
  712.3 5.7 copy-start.81
  712.3 1446.2 %all-reduce.16.cloned.1.call-start = ((), (), s32[]{:S(2)}) async-start(), calls=%async_computation.23 | async-start | bytes 51380224 | tf_op jit(solution)/shard_map/psum | solution.py:318
  712.3 5.7 copy-start.76
  724.4 7.5 copy-start.29
  724.4 7.5 copy-start.41
  724.4 7.5 copy-start.43
  724.4 7.5 copy-start.74
  738.5 6.8 copy-start.36
  753.3 243.9 %copy-start.17 = (bf16[128,2048]{1,0:T(8,128)(2,1)S(1)}, bf16[128,2048]{1,0:T(8,128)(2,1)}, u32[]{:S(2)}) copy-start(bf16[128,2048]{1,0:T(8,128)(2,1)} %param.18) | copy-start | bytes 1572868
  753.3 243.9 %copy-start.49 = (f32[8,1,256]{2,1,0:T(1,128)S(1)}, f32[8,1,256]{2,1,0:T(1,128)}, u32[]{:S(2)}) copy-start(f32[8,1,256]{2,1,0:T(1,128)} %copy-done.48) | copy-start | bytes 24580
  753.3 243.9 %copy-start.59 = (f32[128]{0:T(128)S(1)}, f32[128]{0:T(128)}, u32[]{:S(2)}) copy-start(f32[128]{0:T(128)} %copy-done.58) | copy-start | bytes 1540
  753.3 245.5 %copy-start.52 = (f32[2048]{0:T(1024)S(1)}, f32[2048]{0:T(1024)}, u32[]{:S(2)}) copy-start(f32[2048]{0:T(1024)} %get-tuple-element.223) | copy-start | bytes 24580
  753.3 300.7 %copy-start.7 = (f32[128,2048]{1,0:T(8,128)S(1)}, f32[128,2048]{1,0:T(8,128)}, u32[]{:S(2)}) copy-start(f32[128,2048]{1,0:T(8,128)} %copy-done.5) | copy-start | bytes 3145732
  753.3 300.7 %copy-start.13 = (bf16[128,2048]{1,0:T(8,128)(2,1)S(1)}, bf16[128,2048]{1,0:T(8,128)(2,1)}, u32[]{:S(2)}) copy-start(bf16[128,2048]{1,0:T(8,128)(2,1)} %param.31) | copy-start | bytes 1572868
  753.3 300.7 %copy-start.19 = (f32[128,2048]{1,0:T(8,128)S(1)}, f32[128,2048]{1,0:T(8,128)}, u32[]{:S(2)}) copy-start(f32[128,2048]{1,0:T(8,128)} %copy-done.18) | copy-start | bytes 3145732
  753.3 300.7 %copy-start.47 = (f32[8,1,256]{2,1,0:T(1,128)S(1)}, f32[8,1,256]{2,1,0:T(1,128)}, u32[]{:S(2)}) copy-start(f32[8,1,256]{2,1,0:T(1,128)} %copy-done.45) | copy-start | bytes 24580
  753.3 300.7 %copy-start.56 = (f32[128]{0:T(128)S(1)}, f32[128]{0:T(128)}, u32[]{:S(2)}) copy-start(f32[128]{0:T(128)} %copy-done.54) | copy-start | bytes 1540
  753.4 300.7 %copy-start.61 = (f32[128]{0:T(128)S(1)}, f32[128]{0:T(128)}, u32[]{:S(2)}) copy-start(f32[128]{0:T(128)} %copy-done.60) | copy-start | bytes 1540
  753.4 300.7 %copy-start.66 = (f32[128]{0:T(128)S(1)}, f32[128]{0:T(128)}, u32[]{:S(2)}) copy-start(f32[128]{0:T(128)} %copy-done.65) | copy-start | bytes 1540
  2158.5 6.0 copy-start.39
  2165.9 12.2 copy-start.1
  (48 other events, 92.3 us)
Sparse Core Ops, SparseCore 0:
  22.3 37.0 all-gather.9
  93.5 71.2 reduce-scatter.6
  168.3 36.6 all-gather.15
  207.5 36.7 all-gather.17
  246.2 116.5 all-gather.11
  364.7 67.6 all-gather.13
  436.8 71.3 reduce-scatter.8
  511.6 71.2 reduce-scatter.10
  588.1 36.6 all-gather.19
  636.4 285.9 all-reduce.13
  925.9 71.2 reduce-scatter.12
  1000.9 33.1 reduce-scatter.14
  1037.7 264.3 reduce-scatter.16
  1306.2 852.2 all-reduce.15
where the time goes:
time: 2200 us; the launch traced here: 2190 us
  waiting for transfers between devices  1630 us (74%)
  matrix products  215 us (10%)
  local copies, waits for them, and re-layouts  173 us (8%)
  blocking collectives  80.4 us (4%)
  other arithmetic  49.6 us (2%)
    psum x1, waiting for transfers between devices, per_device(): lax.psum((g_gain_one, grad_qkv, grad_bias, grad_out, g_gain_two, g_router...  847 us
    reduce_scatter x1, waiting for transfers between devices, per_device(): lax.psum_scatter(grad_egu, 'shard', scatter_dimension=0, tiled=True)  244 us
    unnamed x15, waiting for transfers between devices  169 us
    reduce_scatter x1, waiting for transfers between devices, per_device(): lax.psum_scatter(d_in_part, 'shard', scatter_dimension=0, tiled=True)  70.2 us
    reduce_scatter x1, waiting for transfers between devices, per_device(): lax.psum_scatter(attn_part, 'shard', scatter_dimension=0, tiled=True)  61.9 us
    unnamed x170, local copies, waits for them, and re-layouts  58.2 us
  transfers between devices with their start and end apart: 18, of which 15 were waited for; matrix products, arithmetic and copies ran while one was open for 17% of the time, Pallas kernels for 0%

commit v1 on v0

v1 whole, which is shorter than its diff:
```python
import functools
import jax
import jax.numpy as jnp
from jax import lax
from jax.experimental import pallas as pl
from jax.experimental.pallas import tpu as pltpu
from jax.sharding import PartitionSpec as P

HEADS = 16
HEAD_DIM = 128
EXPERT_FF = 1408
TOPK = 4
LANES = 128
EPSILON = 1e-06
ROPE_BASE = 1000000.0
MASKED = -1e30
F32 = jnp.float32
BF16 = jnp.bfloat16
NN = ((1,), (0,))
NT = ((1,), (1,))
TN = ((0,), (0,))
VMEM_LIMIT = 60 << 20


def dot(left, right, dims):
    return lax.dot_general(left, right, (dims, ((), ())), preferred_element_type=F32)


def logistic(values):
    return 1.0 / (1.0 + jnp.exp(-values))


def params(*order):
    return pltpu.CompilerParams(dimension_semantics=order, vmem_limit_bytes=VMEM_LIMIT)


def cost(flops, nbytes, special=0):
    return pl.CostEstimate(flops=int(flops), bytes_accessed=int(nbytes), transcendentals=int(special))


def qkv_body(block, blocks_ref, x_ref, gain_ref, w_ref, bias_ref, cos_ref, sin_ref, qkv_ref, attn_t_ref):
    step = pl.program_id(0)
    x = x_ref[...].astype(F32)
    inv = lax.rsqrt(jnp.mean(x * x, axis=1, keepdims=True) + EPSILON)
    attn_in = (x * inv * gain_ref[...]).astype(BF16)
    attn_t_ref[...] = attn_in.T
    cols = w_ref.shape[2]
    per_step = x.shape[0] // block
    for part in range(3):
        heads = dot(attn_in, w_ref[part], NN) + bias_ref[part : part + 1].astype(F32)
        for b in range(per_step):
            row = pl.multiple_of(blocks_ref[step * per_step + b] * block, block)
            own = heads[b * block : (b + 1) * block]
            if part < 2:
                cosine = cos_ref[pl.ds(row, block)]
                sine = sin_ref[pl.ds(row, block)]
                turned = []
                for h in range(cols // HEAD_DIM):
                    one = own[:, h * HEAD_DIM : (h + 1) * HEAD_DIM]
                    turned.append(one * cosine + pltpu.roll(one, HEAD_DIM // 2, 1) * sine)
                own = jnp.concatenate(turned, 1) if len(turned) > 1 else turned[0]
            qkv_ref[pl.ds(row, block), part * cols : (part + 1) * cols] = own.astype(BF16)


def qkv_forward(x_all, gain, w_three, bias, cosine, sine_signed, blocks, block):
    rows, width = x_all.shape
    cols = w_three.shape[2]
    tile = 2 * block
    whole = lambda *shape: pl.BlockSpec(shape, lambda i, b: (0,) * len(shape))
    return pl.pallas_call(
        functools.partial(qkv_body, block),
        grid_spec=pltpu.PrefetchScalarGridSpec(
            num_scalar_prefetch=1,
            grid=(rows // tile,),
            in_specs=[
                pl.BlockSpec((tile, width), lambda i, b: (i, 0)),
                whole(1, width),
                whole(3, width, cols),
                whole(3, cols),
                whole(rows, HEAD_DIM),
                whole(rows, HEAD_DIM),
            ],
            out_specs=[
                whole(rows, 3 * cols),
                pl.BlockSpec((width, tile), lambda i, b: (0, i)),
            ],
        ),
        out_shape=[
            jax.ShapeDtypeStruct((rows, 3 * cols), BF16),
            jax.ShapeDtypeStruct((width, rows), BF16),
        ],
        compiler_params=params("arbitrary"),
        cost_estimate=cost(6 * rows * width * cols, 4 * rows * width + 6 * width * cols),
        name="qkv_forward",
    )(blocks, x_all, gain, w_three, bias, cosine, sine_signed)


def tile_mask(tile, cont, inside):
    query = lax.broadcasted_iota(jnp.int32, (tile, tile), 0)
    key = lax.broadcasted_iota(jnp.int32, (tile, tile), 1)
    ok = key <= query
    if inside:
        ok = ok & (query // cont == key // cont)
    return ok


def attend_body(block, prompt, blocks_ref, q_ref, k_ref, v_ref, ctx_ref, ctx_t_ref):
    rows = q_ref.shape[0]
    tile = 2 * block
    scale = HEAD_DIM ** (-0.5)
    for t in range(rows // tile):
        at = t * tile
        own = slice(at, at + tile)
        before = min(at, prompt)
        q = q_ref[own]
        near = dot(q, k_ref[own], NT) * scale
        near = jnp.where(tile_mask(tile, block, at >= prompt), near, MASKED)
        if before:
            scores = jnp.concatenate([dot(q, k_ref[:before], NT) * scale, near], 1)
        else:
            scores = near
        top = jnp.max(scores, axis=1, keepdims=True)
        expo = jnp.exp(scores - top)
        probs = (expo / jnp.sum(expo, axis=1, keepdims=True)).astype(BF16)
        mixed = dot(probs[:, before:], v_ref[own], NN)
        if before:
            mixed = mixed + dot(probs[:, :before], v_ref[:before], NN)
        mixed = mixed.astype(BF16)
        mixed_t = mixed.T
        for b in range(2):
            row = pl.multiple_of(blocks_ref[2 * t + b] * block, block)
            ctx_ref[pl.ds(row, block)] = mixed[b * block : (b + 1) * block]
            ctx_t_ref[:, pl.ds(row, block)] = mixed_t[:, b * block : (b + 1) * block]


def attend_forward(qkv, blocks, block, prompt):
    rows = qkv.shape[0]
    heads = qkv.shape[1] // (3 * HEAD_DIM)
    spec = lambda off: pl.BlockSpec((rows, HEAD_DIM), lambda h, b: (0, off + h))
    return pl.pallas_call(
        functools.partial(attend_body, block, prompt),
        grid_spec=pltpu.PrefetchScalarGridSpec(
            num_scalar_prefetch=1,
            grid=(heads,),
            in_specs=[spec(0), spec(heads), spec(2 * heads)],
            out_specs=[spec(0), pl.BlockSpec((HEAD_DIM, rows), lambda h, b: (h, 0))],
        ),
        out_shape=[
            jax.ShapeDtypeStruct((rows, heads * HEAD_DIM), BF16),
            jax.ShapeDtypeStruct((heads * HEAD_DIM, rows), BF16),
        ],
        compiler_params=params("arbitrary"),
        cost_estimate=cost(2.4 * rows * rows * heads * HEAD_DIM, 8 * rows * heads * HEAD_DIM, rows * rows * heads * 0.6),
        name="attend_forward",
    )(blocks, qkv, qkv, qkv)


def attend_back_body(block, prompt, blocks_ref, q_ref, k_ref, v_ref, g_ref, cos_ref, sin_ref, out_ref, dk_ref, dv_ref):
    rows = q_ref.shape[0]
    tile = 2 * block
    half = HEAD_DIM // 2
    scale = HEAD_DIM ** (-0.5)
    dk_ref[...] = jnp.zeros_like(dk_ref)
    dv_ref[...] = jnp.zeros_like(dv_ref)

    def store(part, at, value):
        for b in range(2):
            row = pl.multiple_of(blocks_ref[at // block + b] * block, block)
            out_ref[part, pl.ds(row, block)] = value[b * block : (b + 1) * block].astype(BF16)

    def unturn(value, at):
        cosine = cos_ref[at : at + tile]
        scaled = value * sin_ref[at : at + tile]
        return value * cosine + pltpu.roll(scaled, half, 1)

    for t in range(rows // tile):
        at = t * tile
        own = slice(at, at + tile)
        before = min(at, prompt)
        q = q_ref[own]
        grads = []
        for b in range(2):
            row = pl.multiple_of(blocks_ref[2 * t + b] * block, block)
            grads.append(g_ref[pl.ds(row, block)])
        g = jnp.concatenate(grads, 0)
        key = lax.broadcasted_iota(jnp.int32, (tile, tile), 0)
        query = lax.broadcasted_iota(jnp.int32, (tile, tile), 1)
        ok = key <= query
        if at >= prompt:
            ok = ok & (query // block == key // block)
        near = jnp.where(ok, dot(k_ref[own], q, NT) * scale, MASKED)
        d_near = dot(v_ref[own], g, NT)
        if before:
            scores = jnp.concatenate([dot(k_ref[:before], q, NT) * scale, near], 0)
            d_probs = jnp.concatenate([dot(v_ref[:before], g, NT), d_near], 0)
        else:
            scores, d_probs = near, d_near
        top = jnp.max(scores, axis=0, keepdims=True)
        expo = jnp.exp(scores - top)
        probs = expo / jnp.sum(expo, axis=0, keepdims=True)
        delta = jnp.sum(d_probs * probs, axis=0, keepdims=True)
        d_scores = (probs * (d_probs - delta)).astype(BF16)
        probs = probs.astype(BF16)
        dq = dot(d_scores[before:], k_ref[own], TN)
        if before:
            dq = dq + dot(d_scores[:before], k_ref[:before], TN)
            dk_ref[:before] += dot(d_scores[:before], q, NN)
            dv_ref[:before] += dot(probs[:before], g, NN)
        dk_ref[own] += dot(d_scores[before:], q, NN)
        dv_ref[own] += dot(probs[before:], g, NN)
        store(0, at, unturn(dq * scale, at))
    for t in range(rows // tile):
        at = t * tile
        own = slice(at, at + tile)
        store(1, at, unturn(dk_ref[own] * scale, at))
        store(2, at, dv_ref[own])


def attend_backward(qkv, d_ctx, cosine, sine_back, blocks, block, prompt):
    rows = qkv.shape[0]
    heads = qkv.shape[1] // (3 * HEAD_DIM)
    spec = lambda off: pl.BlockSpec((rows, HEAD_DIM), lambda h, b: (0, off + h))
    table = pl.BlockSpec((rows, HEAD_DIM), lambda h, b: (0, 0))
    return pl.pallas_call(
        functools.partial(attend_back_body, block, prompt),
        grid_spec=pltpu.PrefetchScalarGridSpec(
            num_scalar_prefetch=1,
            grid=(heads,),
            in_specs=[spec(0), spec(heads), spec(2 * heads), spec(0), table, table],
            out_specs=pl.BlockSpec((3, rows, HEAD_DIM), lambda h, b: (0, 0, h)),
            scratch_shapes=[pltpu.VMEM((rows, HEAD_DIM), F32)] * 2,
        ),
        out_shape=jax.ShapeDtypeStruct((3, rows, heads * HEAD_DIM), BF16),
        compiler_params=params("arbitrary"),
        cost_estimate=cost(6 * rows * rows * heads * HEAD_DIM, 16 * rows * heads * HEAD_DIM, rows * rows * heads * 0.6),
        name="attend_backward",
    )(blocks, qkv, qkv, qkv, d_ctx, cosine, sine_back)


def input_grad_body(d_ref, w_ref, out_ref):
    total = dot(d_ref[0], w_ref[0], NT)
    for part in range(1, 3):
        total = total + dot(d_ref[part], w_ref[part], NT)
    out_ref[...] = total.astype(BF16)


def input_grad(d_qkv, w_three):
    _, rows, cols = d_qkv.shape
    width = w_three.shape[1]
    tile = 256
    return pl.pallas_call(
        input_grad_body,
        grid=(rows // tile,),
        in_specs=[
            pl.BlockSpec((3, tile, cols), lambda i: (0, i, 0)),
            pl.BlockSpec((3, width, cols), lambda i: (0, 0, 0)),
        ],
        out_specs=pl.BlockSpec((tile, width), lambda i: (i, 0)),
        out_shape=jax.ShapeDtypeStruct((rows, width), BF16),
        compiler_params=params("arbitrary"),
        cost_estimate=cost(6 * rows * width * cols, 2 * rows * width + 6 * width * cols),
        name="input_grad",
    )(d_qkv, w_three)


def shared_body(x_ref, dy_ref, wz_ref, w_ref, back_ref, out_ref, d_so_ref, sh_t_ref, dg_t_ref, du_t_ref):
    x = x_ref[...]
    dy = dy_ref[...].astype(F32)
    z = logistic(jnp.sum(x.astype(F32) * wz_ref[...], axis=1, keepdims=True))
    d_so = (z * dy).astype(BF16)
    d_so_ref[...] = d_so
    gate = dot(x, w_ref[0], NT)
    up = dot(x, w_ref[1], NT)
    sig = logistic(gate)
    act = gate * sig
    hidden = (act * up).astype(BF16)
    sh_t_ref[...] = hidden.T
    d_sh = dot(d_so, w_ref[2], NT)
    d_gate = (d_sh * up * (sig * (1.0 + gate * (1.0 - sig)))).astype(BF16)
    d_up = (d_sh * act).astype(BF16)
    dg_t_ref[...] = d_gate.T
    du_t_ref[...] = d_up.T
    width = x.shape[1]
    back_ref[:, :width] = (dot(d_gate, w_ref[0], NN) + dot(d_up, w_ref[1], NN)).astype(BF16)
    out = dot(hidden, w_ref[2], NN)
    out_ref[...] = out.astype(BF16)
    dz = jnp.sum(dy * out, axis=1, keepdims=True)
    lane = lax.broadcasted_iota(jnp.int32, (x.shape[0], LANES), 1)
    back_ref[:, width:] = jnp.where(lane == 0, dz, 0.0).astype(BF16)


def shared_expert(x_all, dy_all, wz, w_three):
    rows, width = x_all.shape
    ff = w_three.shape[1]
    tile = 256
    row_spec = pl.BlockSpec((tile, width), lambda i: (i, 0))
    col_spec = pl.BlockSpec((ff, tile), lambda i: (0, i))
    return pl.pallas_call(
        shared_body,
        grid=(rows // tile,),
        in_specs=[
            row_spec,
            row_spec,
            pl.BlockSpec((1, width), lambda i: (0, 0)),
            pl.BlockSpec((3, ff, width), lambda i: (0, 0, 0)),
        ],
        out_specs=[
            pl.BlockSpec((tile, width + LANES), lambda i: (i, 0)),
            row_spec,
            row_spec,
            col_spec,
            col_spec,
            col_spec,
        ],
        out_shape=[jax.ShapeDtypeStruct((rows, width + LANES), BF16)]
        + [jax.ShapeDtypeStruct((rows, width), BF16)] * 2
        + [jax.ShapeDtypeStruct((ff, rows), BF16)] * 3,
        compiler_params=params("arbitrary"),
        cost_estimate=cost(12 * rows * width * ff, 10 * rows * width + 6 * width * ff + 6 * rows * ff, rows * ff),
        name="shared_expert",
    )(x_all, dy_all, wz, w_three)


def expert_chunks(ff):
    edges = list(range(0, ff, 256)) + [ff]
    return list(zip(edges[:-1], edges[1:]))


def expert_body(
    meta_ref, place_ref, x_all_ref, dy_all_ref, router_ref, gu_hbm, down_hbm,
    back_ref, routed_ref, d_both_ref, x_t_ref, h_t_ref, d_out_ref,
    gu, down, x_ref, dy_ref, weight_ref, out_acc, in_acc, sems,
):
    ff = EXPERT_FF
    step = pl.program_id(0)
    last = pl.num_programs(0) - 1
    sources, tokens, width = x_all_ref.shape
    slots = x_ref.shape[0] // sources
    shards, _, gu_rows, _ = gu_hbm.shape
    down_rows = down_hbm.shape[2]
    spans = expert_chunks(ff)
    expert = meta_ref[0] * pl.num_programs(0) + step

    def copies(which, at, lo, hi):
        return [
            pltpu.make_async_copy(
                gu_hbm.at[:, which, :, pl.ds(base, hi - lo)],
                gu.at[:, :, pl.ds(base, hi - lo)],
                sems.at[2 * at + part],
            )
            for part, base in enumerate((lo, ff + lo))
        ]

    def down_copies(which):
        return [
            pltpu.make_async_copy(
                down_hbm.at[s, which],
                down.at[pl.ds(s * down_rows, down_rows)],
                sems.at[2 * len(spans) + s],
            )
            for s in range(shards)
        ]

    @pl.when(step == 0)
    def _():
        for at, (lo, hi) in enumerate(spans):
            for copy in copies(0, at, lo, hi):
                copy.start()
            if at == 0:
                for copy in down_copies(0):
                    copy.start()
        back_ref[...] = jnp.zeros_like(back_ref)
        routed_ref[...] = jnp.zeros_like(routed_ref)

    slot_line = lax.broadcasted_iota(jnp.int32, (slots, tokens), 0)

    def chosen(k):
        return slot_line == place_ref[0, k : k + 1, :]

    for k in range(sources):
        rows = slice(k * slots, (k + 1) * slots)
        mask = chosen(k)
        one_hot = jnp.where(mask, 1.0, 0.0).astype(BF16)
        source = x_all_ref[k]
        x_ref[rows] = dot(one_hot, source, NN).astype(BF16)
        dy_ref[rows] = dot(one_hot, dy_all_ref[k], NN).astype(BF16)
        logits = dot(router_ref[...], source, NT)
        expo = jnp.exp(logits - jnp.max(logits, axis=0, keepdims=True))
        router = expo / jnp.sum(expo, axis=0, keepdims=True)
        own = lax.broadcasted_iota(jnp.int32, router.shape, 0) == expert
        own = jnp.sum(jnp.where(own, router, 0.0), axis=0, keepdims=True)
        weight_ref[rows] = jnp.sum(jnp.where(mask, own, 0.0), axis=1, keepdims=True)
    x = x_ref[...]
    weight = weight_ref[...]
    d_out = (weight * dy_ref[...].astype(F32)).astype(BF16)
    d_out_ref[0] = d_out
    x_t_ref[0] = x.T
    for at, (lo, hi) in enumerate(spans):
        for copy in copies(0, at, lo, hi):
            copy.wait()
        if at == 0:
            for copy in down_copies(0):
                copy.wait()
        w_gate = gu[:, :, lo:hi].reshape(width, hi - lo)
        w_up = gu[:, :, ff + lo : ff + hi].reshape(width, hi - lo)
        w_down = down[lo:hi]
        gate = dot(x, w_gate, NN)
        up = dot(x, w_up, NN)
        sig = logistic(gate)
        act = gate * sig
        hidden = (act * up).astype(BF16)
        h_t_ref[0, lo:hi] = hidden.T
        d_h = dot(d_out, w_down, NT)
        d_gate = (d_h * up * (sig * (1.0 + gate * (1.0 - sig)))).astype(BF16)
        d_up = (d_h * act).astype(BF16)
        d_both_ref[0, :, lo:hi] = d_gate
        d_both_ref[0, :, ff + lo : ff + hi] = d_up
        out_new = dot(hidden, w_down, NN)
        in_new = dot(d_gate, w_gate, NT) + dot(d_up, w_up, NT)
        if at == 0:
            out_acc[...] = out_new
            in_acc[...] = in_new
        else:
            out_acc[...] += out_new
            in_acc[...] += in_new

        @pl.when(step < last)
        def _():
            for copy in copies(step + 1, at, lo, hi):
                copy.start()
            if at == len(spans) - 1:
                for copy in down_copies(step + 1):
                    copy.start()

    e_out = out_acc[...].astype(BF16).astype(F32)
    d_weight = jnp.sum(dy_ref[...].astype(F32) * e_out, axis=1, keepdims=True)
    mixed = (weight * e_out).astype(BF16)
    d_in = in_acc[...].astype(BF16)
    lane = lax.broadcasted_iota(jnp.int32, (slots, LANES), 1)
    for k in range(sources):
        rows = slice(k * slots, (k + 1) * slots)
        one_hot = jnp.where(chosen(k), 1.0, 0.0).astype(BF16)
        spread = jnp.where(lane == expert, d_weight[rows], 0.0).astype(BF16)
        for ref, cols, value in (
            (routed_ref, slice(0, width), mixed[rows]),
            (back_ref, slice(0, width), d_in[rows]),
            (back_ref, slice(width, width + LANES), spread),
        ):
            so_far = ref[k, :, cols].astype(F32)
            ref[k, :, cols] = (so_far + dot(one_hot, value, TN)).astype(BF16)


def expert_pass(place, x_all, dy_all, w_router, gate_up, down, expert_at, slots):
    sources, tokens, width = x_all.shape
    local = gate_up.shape[1]
    ff = EXPERT_FF
    rows = sources * slots
    n = len(expert_chunks(ff))
    once = lambda *shape: pl.BlockSpec(
        shape, lambda e, m: (0,) * len(shape), pipeline_mode=pl.Buffered(1)
    )
    each = lambda *shape: pl.BlockSpec((1,) + shape, lambda e, m: (e,) + (0,) * len(shape))
    hbm = pl.BlockSpec(memory_space=pl.ANY)
    return pl.pallas_call(
        expert_body,
        grid_spec=pltpu.PrefetchScalarGridSpec(
            num_scalar_prefetch=1,
            grid=(local,),
            in_specs=[
                each(sources, tokens),
                once(sources, tokens, width),
                once(sources, tokens, width),
                once(*w_router.shape),
                hbm,
                hbm,
            ],
            out_specs=[
                once(sources, tokens, width + LANES),
                once(sources, tokens, width),
                each(rows, 2 * ff),
                each(width, rows),
                each(ff, rows),
                each(rows, width),
            ],
            scratch_shapes=[
                pltpu.VMEM((gate_up.shape[0], gate_up.shape[2], 2 * ff), BF16),
                pltpu.VMEM((ff, width), BF16),
                pltpu.VMEM((rows, width), BF16),
                pltpu.VMEM((rows, width), BF16),
                pltpu.VMEM((rows, 1), F32),
                pltpu.VMEM((rows, width), F32),
                pltpu.VMEM((rows, width), F32),
                pltpu.SemaphoreType.DMA((2 * n + gate_up.shape[0],)),
            ],
        ),
        out_shape=[
            jax.ShapeDtypeStruct((sources, tokens, width + LANES), BF16),
            jax.ShapeDtypeStruct((sources, tokens, width), BF16),
            jax.ShapeDtypeStruct((local, rows, 2 * ff), BF16),
            jax.ShapeDtypeStruct((local, width, rows), BF16),
            jax.ShapeDtypeStruct((local, ff, rows), BF16),
            jax.ShapeDtypeStruct((local, rows, width), BF16),
        ],
        compiler_params=params("arbitrary"),
        cost_estimate=cost(
            12 * local * rows * width * ff,
            local * (6 * width * ff + 8 * rows * width + 6 * rows * ff),
            local * rows * ff,
        ),
        name="expert_pass",
    )(expert_at.reshape(1), place, x_all, dy_all, w_router, gate_up, down)


def rope_tables(positions):
    half = HEAD_DIM // 2
    freq = ROPE_BASE ** (-jnp.arange(half, dtype=F32) * 2.0 / HEAD_DIM)
    angle_tab = positions.astype(F32)[:, None] * freq[None, :]
    cosine = jnp.cos(angle_tab)
    sine = jnp.sin(angle_tab)
    return (jnp.concatenate([cosine, cosine], 1), jnp.concatenate([-sine, sine], 1))


def softmax_rows(scores):
    top = jnp.max(scores, axis=-1, keepdims=True)
    expo = jnp.exp(scores - top)
    return expo / jnp.sum(expo, axis=-1, keepdims=True)


def after(value, *others):
    return lax.optimization_barrier((value,) + others)[0]


def add(left, right):
    return left.astype(F32) + right.astype(F32)


def swap(array, bits, axis="shard"):
    count = lax.axis_size(axis)
    return lax.ppermute(array, axis, [(i, i ^ bits) for i in range(count)])


def gather_shard(array):
    if lax.axis_size("shard") != 8:
        return lax.all_gather(array, "shard", axis=0, tiled=True), array
    half = array.shape[0] // 2
    top, low = array[:half], array[half:]
    top_x = swap(top, 2)
    low_y = swap(low, 4)
    own_c = swap(array, 1)
    top_y2 = swap(jnp.concatenate([top, top_x], 0), 4)
    low_x2 = swap(jnp.concatenate([low, low_y], 0), 2)
    near_c = swap(jnp.concatenate([top_x, low_y], 0), 1)
    far_c = swap(jnp.concatenate([top_y2, low_x2], 0), 1)
    top_y, top_xy = top_y2[:half], top_y2[half:]
    low_x, low_xy = low_x2[:half], low_x2[half:]
    top_xc, low_yc = near_c[:half], near_c[half:]
    top_yc, top_xyc, low_xc, low_xyc = [far_c[i * half : (i + 1) * half] for i in range(4)]
    joined = jnp.concatenate(
        [array, own_c, top_x, low_x, top_xc, low_xc, top_y, low_y, top_yc, low_yc]
        + [top_xy, low_xy, top_xyc, low_xyc],
        0,
    )
    return joined, top_x


def gather_small(array):
    if lax.axis_size("shard") != 8:
        return lax.all_gather(array, "shard", axis=0, tiled=False)
    parts = array[None]
    for bits in (1, 2, 4):
        parts = jnp.concatenate([parts, swap(parts, bits)], 0)
    return reorder(parts)


def block_of():
    order = jnp.arange(lax.axis_size("shard"), dtype=jnp.int32)
    return lax.axis_index("shard") ^ order if lax.axis_size("shard") == 8 else order


def reorder(array):
    if lax.axis_size("shard") != 8:
        return array
    own = lax.axis_index("shard")
    return jnp.concatenate([lax.dynamic_slice_in_dim(array, own ^ r, 1, 0) for r in range(8)], 0)


def scatter_shard(blocks):
    if lax.axis_size("shard") != 8:
        return lax.psum_scatter(blocks, "shard", scatter_dimension=0, tiled=False).astype(F32)
    cut = blocks.reshape((2, 2, 2) + blocks.shape[1:])
    both = add(cut[:, :, 0], swap(cut[:, :, 1], 1)).astype(BF16)
    half = blocks.shape[1] // 2
    top, low = both[:, :, :half], both[:, :, half:]
    top = add(top[:, 0], swap(top[:, 1], 2)).astype(BF16)
    low = add(low[0], swap(low[1], 4)).astype(BF16)
    top = add(top[0], swap(top[1], 4))
    low = add(low[0], swap(low[1], 2))
    return jnp.concatenate([top, low], 0)


def turn(array, step):
    count = lax.axis_size("expert")
    return lax.ppermute(array, "expert", [(i, (i + step) % count) for i in range(count)])


def gather_expert(array):
    return jnp.stack([array] + [turn(array, k) for k in range(1, lax.axis_size("expert"))], 0)


def return_expert(blocks):
    total = blocks[0].astype(F32)
    for k in range(1, lax.axis_size("expert")):
        total = total + turn(blocks[k], -k).astype(F32)
    return total


def sum_small(array, *axes):
    for axis in axes:
        bits = 1
        while bits < lax.axis_size(axis):
            array = array + swap(array, bits, axis)
            bits *= 2
    return array


def sum_expert(pieces):
    if lax.axis_size("expert") != 4:
        return [lax.psum(piece, "expert").astype(F32) for piece in pieces]
    place = lax.axis_index("expert")
    inner = (place == 1) | (place == 2)
    sums, before = [], None
    for piece in pieces:
        outer = lax.ppermute(piece, "expert", [(0, 1), (3, 2)])
        if before is not None:
            outer = after(outer, before)
        side = add(piece, outer).astype(BF16)
        other = lax.ppermute(side, "expert", [(1, 2), (2, 1)])
        total = add(side, other).astype(BF16)
        before = total
        back = lax.ppermute(total, "expert", [(1, 0), (2, 3)])
        sums.append(jnp.where(inner, total, back).astype(F32))
    return sums


def per_device(
    tokens,
    attn_gain,
    qkv_weight,
    qkv_bias,
    out_weight,
    ffn_gain,
    router_weight,
    shared_gate_weight,
    shared_weights,
    expert_gate_up,
    expert_down,
    routes,
    arrival,
    cotangent,
):
    shard_count = lax.axis_size("shard")
    expert_count = lax.axis_size("expert")
    shard_at = lax.axis_index("shard")
    expert_at = lax.axis_index("expert")
    rows_local = tokens.shape[0]
    width = tokens.shape[1]
    group_rows = rows_local * shard_count
    prompt_len = group_rows // 2
    local_experts = expert_gate_up.shape[1]
    experts_all = local_experts * expert_count
    capacity = rows_local * TOPK // experts_all
    blocks = block_of()

    tokens_all, started = gather_shard(tokens)
    params_own = jnp.concatenate(
        [attn_gain[None], ffn_gain[None], shared_gate_weight[None], router_weight.T], 0
    )
    params_all = jnp.moveaxis(gather_small(params_own), 0, 1).reshape(-1, width)
    gain_one_f = params_all[0:1].astype(F32)
    gain_two_f = params_all[1:2].astype(F32)
    w_zgate = params_all[2:3]
    w_router = params_all[3:]

    gate_up_own = jnp.moveaxis(after(expert_gate_up, started), 1, 0)
    down_own = jnp.moveaxis(after(expert_down, started), 1, 0)
    w_gate_up = lax.all_gather(gate_up_own, "shard", axis=0, tiled=False)
    w_down = lax.all_gather(down_own, "shard", axis=0, tiled=False)

    route_flat = routes.reshape(-1)
    priority = arrival.reshape(-1)
    same_expert = route_flat[:, None] == route_flat[None, :]
    earlier = priority[None, :] < priority[:, None]
    ranks = jnp.sum((same_expert & earlier).astype(jnp.int32), axis=1)
    kept_rank = jnp.where(ranks < capacity, ranks + 1, 0).reshape(rows_local, TOPK)
    expert_ids = jnp.arange(experts_all, dtype=jnp.int32)
    place = (
        jnp.sum(
            jnp.where(routes[:, :, None] == expert_ids[None, None, :], kept_rank[:, :, None], 0), 1
        )
        - 1
    )
    place_z = gather_expert(place.T)
    place_own = jnp.moveaxis(
        lax.dynamic_slice_in_dim(place_z, expert_at * local_experts, local_experts, 1), 1, 0
    )
    dy_z = gather_expert(cotangent)
    dy_all, _ = gather_shard(after(cotangent, tokens_all))

    line = jnp.arange(group_rows, dtype=jnp.int32)
    position = jnp.where(line < prompt_len, line, prompt_len + (line - prompt_len) % rows_local)
    cosine, sine = rope_tables(position)
    w_three = jnp.swapaxes(qkv_weight, 0, 1)
    qkv, attn_t = qkv_forward(
        tokens_all, gain_one_f, w_three, qkv_bias, cosine, sine, blocks, rows_local
    )
    context, context_t = attend_forward(qkv, blocks, rows_local, prompt_len)
    attn_part = dot(context, out_weight, NN).astype(BF16)
    x_float = tokens.astype(F32)
    hidden_state = x_float + scatter_shard(attn_part.reshape(shard_count, rows_local, width))

    inv_two = lax.rsqrt(jnp.mean(hidden_state * hidden_state, axis=1, keepdims=True) + EPSILON)
    normed_two = hidden_state * inv_two
    ffn_in = (normed_two * gain_two_f).astype(BF16)
    ffn_all, _ = gather_shard(ffn_in)
    ffn_z = gather_expert(ffn_in)
    router = softmax_rows(dot(ffn_in, w_router, NT))
    w_zgate_f = w_zgate.astype(F32)
    z_gate = logistic(jnp.sum(ffn_in.astype(F32) * w_zgate_f, axis=1, keepdims=True))
    d_out = cotangent.astype(F32)

    w_shared = jnp.swapaxes(shared_weights, 1, 2)
    shared_back, out_part, d_so, hidden_t, d_gate_t, d_up_t = shared_expert(
        ffn_all, dy_all, w_zgate_f, w_shared
    )
    shared_back = scatter_shard(shared_back.reshape(shard_count, rows_local, width + LANES))
    grad_shared = [
        dot(d_gate_t, ffn_all, NN).astype(BF16),
        dot(d_up_t, ffn_all, NN).astype(BF16),
        dot(hidden_t, d_so, NN).astype(BF16),
    ]
    shared_out = lax.psum_scatter(
        reorder(out_part.reshape(shard_count, rows_local, width)),
        "shard",
        scatter_dimension=0,
        tiled=False,
    )

    routed_back, routed, d_both, x_t, h_t, d_eout = expert_pass(
        place_own, ffn_z, dy_z, w_router, w_gate_up, w_down, expert_at, capacity
    )
    routed_back = return_expert(routed_back)
    routed = return_expert(routed)
    output = (hidden_state + routed + z_gate * shared_out.astype(F32)).astype(BF16)
    grad_gate_up = [dot(x_t[e], d_both[e], NN).astype(BF16) for e in range(local_experts)]
    grad_down = [dot(h_t[e], d_eout[e], NN).astype(BF16) for e in range(local_experts)]

    d_router = routed_back[:, width : width + experts_all]
    d_logit = (router * (d_router - jnp.sum(d_router * router, axis=1, keepdims=True))).astype(BF16)
    grad_router = dot(d_logit, ffn_in, TN)
    d_zlogit = shared_back[:, width : width + 1] * z_gate * (1.0 - z_gate)
    grad_zgate = jnp.sum(d_zlogit * ffn_in.astype(F32), axis=0)
    d_ffn = (
        shared_back[:, :width]
        + routed_back[:, :width]
        + dot(d_logit, w_router, NN)
        + d_zlogit * w_zgate_f
    )
    grad_gain_two = jnp.sum(d_ffn * normed_two, axis=0)
    d_norm_two = d_ffn * gain_two_f
    d_hidden = d_out + inv_two * (
        d_norm_two - normed_two * jnp.mean(d_norm_two * normed_two, axis=1, keepdims=True)
    )
    d_ao_all, _ = gather_shard(d_hidden.astype(BF16))

    d_ctx = dot(d_ao_all, out_weight, NT).astype(BF16)
    d_qkv = attend_backward(qkv, d_ctx, cosine, sine, blocks, rows_local, prompt_len)
    d_in_part = input_grad(d_qkv, w_three)
    d_attn_in = scatter_shard(d_in_part.reshape(shard_count, rows_local, width))
    grad_out = dot(context_t, d_ao_all, NN).astype(BF16)
    grad_qkv = [dot(attn_t, d_qkv[part], NN).astype(BF16) for part in range(3)]
    grad_bias = jnp.sum(d_qkv.astype(F32), axis=1)
    inv_one = lax.rsqrt(jnp.mean(x_float * x_float, axis=1, keepdims=True) + EPSILON)
    normed_one = x_float * inv_one
    grad_gain_one = jnp.sum(d_attn_in * normed_one, axis=0)
    d_norm_one = d_attn_in * gain_one_f
    tokens_grad = (
        d_hidden
        + inv_one
        * (d_norm_one - normed_one * jnp.mean(d_norm_one * normed_one, axis=1, keepdims=True))
    ).astype(BF16)

    g_egu = jnp.stack(
        [lax.psum_scatter(g, "shard", scatter_dimension=0, tiled=True) for g in grad_gate_up], 1
    ).astype(F32)
    g_edown = jnp.stack(
        [lax.psum_scatter(g, "shard", scatter_dimension=0, tiled=True) for g in grad_down], 1
    ).astype(F32)
    s_down, s_gate, s_up, g_out, g_q, g_k, g_v = sum_expert(
        [grad_shared[2], grad_shared[0], grad_shared[1], grad_out] + grad_qkv
    )
    g_shared = jnp.swapaxes(jnp.stack([s_gate, s_up, s_down]), 1, 2)
    g_qkv = jnp.swapaxes(jnp.stack([g_q, g_k, g_v]), 0, 1)
    own_cols = lambda a: lax.dynamic_slice_in_dim(
        a, shard_at * (width // shard_count), width // shard_count, 1
    )
    small = own_cols(
        sum_small(
            jnp.concatenate([grad_router, grad_zgate[None], grad_gain_two[None]], 0),
            "shard",
            "expert",
        )
    )
    g_router = small[:experts_all].T
    g_zgate = small[experts_all]
    g_gain_two = small[experts_all + 1]
    g_gain_one = own_cols(sum_small(grad_gain_one[None], "shard", "expert"))[0]
    g_bias = sum_small(grad_bias, "expert")
    return (
        output,
        tokens_grad,
        g_gain_one,
        g_qkv,
        g_bias,
        g_out,
        g_gain_two,
        g_router,
        g_zgate,
        g_shared,
        g_egu,
        g_edown,
    )


def solution(mesh):
    placed = (
        P(("expert", "shard"), None),
        P("shard"),
        P(None, None, "shard"),
        P(None, "shard"),
        P("shard", None),
        P("shard"),
        P("shard", None),
        P("shard"),
        P(None, None, "shard"),
        P("shard", "expert", None),
        P("shard", "expert", None),
        P(("expert", "shard"), None),
        P(("expert", "shard"), None),
        P(("expert", "shard"), None),
    )
    return jax.shard_map(
        per_device,
        mesh=mesh,
        in_specs=placed,
        out_specs=(
            P(("expert", "shard"), None),
            P(("expert", "shard"), None),
            P("shard"),
            P(None, None, "shard"),
            P(None, "shard"),
            P("shard", None),
            P("shard"),
            P("shard", None),
            P("shard"),
            P(None, None, "shard"),
            P("shard", "expert", None),
            P("shard", "expert", None),
        ),
        check_vma=False,
    )
```

time: 2200 us -> 1210 us (0.55)
  waiting for transfers between devices: 1630 us -> 716 us
  matrix products: 215 us -> 52.5 us
  starting transfers between devices: 19.4 us -> 150 us
  Pallas kernels: 0 us -> 104 us
  local copies, waits for them, and re-layouts: 173 us -> 72.8 us
  blocking collectives: 80.4 us -> 0 us
  other arithmetic: 49.6 us -> 90.8 us
    psum x1 -> x0, waiting for transfers between devices: 847 us -> none  [per_device(): lax.psum((g_gain_one, grad_qkv, grad_bias, grad_out, g_gain_two, g_router...]
    ppermute x0 -> x94, waiting for transfers between devices: none -> 716 us  [the longest x7 239 us: sum_expert(): back = lax.ppermute(total, 'expert', [(1, 0), (2, 3)])]
    reduce_scatter x6 -> x5, waiting for transfers between devices: 389 us -> 0.01 us  [the longest x4 0.01 us: per_device(): lax.psum_scatter(g, 'shard', scatter_dimension=0, tiled=True)]
    unnamed x15 -> x7, waiting for transfers between devices: 169 us -> 0.11 us
    dot_general x40 -> x16, matrix products: 215 us -> 52.5 us  [dot(): lax.dot_general(left, right, (dims, ((), ())), preferred_element_type=F32)]
    ppermute x0 -> x94, starting transfers between devices: none -> 149 us  [the longest x58 57.6 us: swap(): return lax.ppermute(array, axis, [(i, i ^ bits) for i in range(count)])]
    all_to_all x4 -> x0, waiting for transfers between devices: 116 us -> none  [the longest x1 33.1 us: per_device(): lax.all_to_all(e_out[None], 'expert', split_axis=2, concat_axis=0, tiled=...]
    all_gather x6 -> x2, waiting for transfers between devices: 109 us -> 0.01 us  [the longest x1 0.01 us: per_device(): w_down = lax.all_gather(down_own, 'shard', axis=0, tiled=False)]
  transfers between devices with their start and end apart: 18 -> 101, of which waited for: 15 -> 51; matrix products, arithmetic and copies ran while one was open for 17% -> 17% of each run, Pallas kernels for 0% -> 9%
where the time goes in v1:
time: 1210 us; the launch traced here: 1200 us
  waiting for transfers between devices  716 us (59%)
  starting transfers between devices  150 us (12%)
  Pallas kernels  104 us (9%)
  other arithmetic  90.8 us (8%)
  local copies, waits for them, and re-layouts  72.8 us (6%)
  matrix products  52.5 us (4%)
  between operations  15.9 us (1%)
    ppermute x7, waiting for transfers between devices, sum_expert(): back = lax.ppermute(total, 'expert', [(1, 0), (2, 3)])  239 us
    ppermute x58, waiting for transfers between devices, swap(): return lax.ppermute(array, axis, [(i, i ^ bits) for i in range(count)])  189 us
    ppermute x7, waiting for transfers between devices, sum_expert(): outer = lax.ppermute(piece, 'expert', [(0, 1), (3, 2)])  167 us
    ppermute x15, waiting for transfers between devices, turn(): lax.ppermute(array, 'expert', [(i, (i + step) % count) for i in range(cou...  121 us
    ppermute x58, starting transfers between devices, swap(): return lax.ppermute(array, axis, [(i, i ^ bits) for i in range(count)])  57.6 us
    dot_general x16, matrix products, dot(): lax.dot_general(left, right, (dims, ((), ())), preferred_element_type=F32)  52.5 us
    unnamed x158, local copies, waits for them, and re-layouts  52.3 us
    ppermute x7, starting transfers between devices, sum_expert(): outer = lax.ppermute(piece, 'expert', [(0, 1), (3, 2)])  50.7 us
  transfers between devices with their start and end apart: 101, of which 51 were waited for; matrix products, arithmetic and copies ran while one was open for 17% of the time, Pallas kernels for 9%

profile of v1, /device:TPU:0, one launch (start us, length us, event | category | flops | bytes accessed | tf_op | source)
XLA Modules:
  0.0 1202.4 jit_solution(13228342444524018707)
XLA Ops:
  11.4 6.3 collective-permute-done.1
  20.9 3.8 copy.138
  34.7 4.0 collective-permute-done.9
  43.6 16.7 %collective-permute-done.3 = bf16[128,2048]{1,0:T(8,128)(2,1)S(1)} collective-permute-done((bf16[128,2048]{1,0:T(8,128)(2,1)S(1)}, bf16[128,2048]{1,0:T(8,128)(2,1)S(1)}, u32[]{:S(2)}, u32[]{:S(2)}) %collective-permute-start.3) | collective-permute-done | bytes 524320 | tf_op jit(solution)/shard_map/ppermute | solution.py:539
  74.0 10.3 qkv_forward.1
  84.3 6.9 attend_forward.1
  96.8 20.2 %collective-permute-done.37 = bf16[128,2048]{1,0:T(8,128)(2,1)S(1)} collective-permute-done((bf16[128,2048]{1,0:T(8,128)(2,1)S(1)}, bf16[128,2048]{1,0:T(8,128)(2,1)S(1)}, u32[]{:S(2)}, u32[]{:S(2)}) %collective-permute-start.37) | collective-permute-done | bytes 524320 | tf_op jit(solution)/shard_map/ppermute | solution.py:539
  123.1 14.8 %collective-permute-done.11 = bf16[2,64,2048]{2,1,0:T(8,128)(2,1)S(1)} collective-permute-done((bf16[2,64,2048]{2,1,0:T(8,128)(2,1)S(1)}, bf16[2,64,2048]{2,1,0:T(8,128)(2,1)S(1)}, u32[]{:S(2)}, u32[]{:S(2)}) %collective-permute-start.11) | collective-permute-done | bytes 524320 | tf_op jit(solution)/shard_map/ppermute | solution.py:539
  142.9 11.2 collective-permute-done.12
  157.5 12.1 %collective-permute-done.28 = bf16[64,2048]{1,0:T(8,128)(2,1)S(1)} collective-permute-done((bf16[64,2048]{1,0:T(8,128)(2,1)S(1)}, bf16[64,2048]{1,0:T(8,128)(2,1)S(1)}, u32[]{:S(2)}, u32[]{:S(2)}) %collective-permute-start.28) | collective-permute-done | bytes 262176 | tf_op jit(solution)/shard_map/ppermute | solution.py:539
  172.9 15.4 %collective-permute-done.30 = bf16[128,2048]{1,0:T(8,128)(2,1)S(1)} collective-permute-done((bf16[128,2048]{1,0:T(8,128)(2,1)S(1)}, bf16[128,2048]{1,0:T(8,128)(2,1)S(1)}, u32[]{:S(2)}, u32[]{:S(2)}) %collective-permute-start.30) | collective-permute-done | bytes 524320 | tf_op jit(solution)/shard_map/ppermute | solution.py:539
  195.4 29.4 %shared_expert.1 = (bf16[1024,2176]{1,0:T(8,128)(2,1)}, bf16[1024,2048]{1,0:T(8,128)(2,1)}, bf16[1024,2048]{1,0:T(8,128)(2,1)}, bf16[704,1024]{1,0:T(8,128)(2,1)...) custom-call(bf16[1024,2048]{1,0:T(8,128)(2,1)} %copy-done.26, bf16[1024,2048]{1,0:T(8,128)(2,1)} %copy-done.25, ...), custom_call_target="tpu_custom_call" | custom-call | flops 17716740096 | bytes 33947648 | tf_op jit(solution)/shard_map/shared_expert/pallas_call | solution.py:298
  243.8 31.0 %collective-permute-done.15 = s32[8,128]{1,0:T(8,128)S(1)} collective-permute-done((s32[8,128]{1,0:T(8,128)S(1)}, s32[8,128]{1,0:T(8,128)S(1)}, u32[]{:S(2)}, u32[]{:S(2)}) %collective-permute-start.15) | collective-permute-done | bytes 4128 | tf_op jit(solution)/shard_map/ppermute | solution.py:603
  274.8 11.2 collective-permute-done.16
  286.5 3.9 collective-permute-start.19
  295.6 7.3 collective-permute-done.18
  302.9 21.3 %collective-permute-done.19 = bf16[128,2048]{1,0:T(8,128)(2,1)} collective-permute-done((bf16[128,2048]{1,0:T(8,128)(2,1)S(1)}, bf16[128,2048]{1,0:T(8,128)(2,1)}, u32[]{:S(2)}, u32[]{:S(2)}) %collective-permute-start.19) | collective-permute-done | bytes 524320 | tf_op jit(solution)/shard_map/ppermute | solution.py:603
  327.1 40.4 %expert_pass.1 = (bf16[4,128,2176]{2,1,0:T(8,128)(2,1)}, bf16[4,128,2048]{2,1,0:T(8,128)(2,1)}, bf16[2,256,2816]{2,1,0:T(8,128)(2,1)}, bf16[2,2048,256]{2,1,0:T(...) custom-call(s32[1]{0:T(128)} %bitcast.16.meta_ref, s32[2,4,128]{2,1,0:T(4,128)} %fusion.61.place_ref, ...), custom_call_target="tpu_custom_call" | custom-call | flops 17716740096 | bytes 47316992 | tf_op jit(solution)/shard_map/expert_pass/pallas_call | solution.py:464
  367.5 5.6 convolution_convert_fusion.3
  373.2 7.5 convolution_convert_fusion.5
  380.7 14.3 %collective-permute-start.70 = (bf16[704,2048]{1,0:T(8,128)(2,1)}, bf16[704,2048]{1,0:T(8,128)(2,1)}, u32[]{:S(2)}, u32[]{:S(2)}) collective-permute-start(bf16[704,2048]{1,0:T(8,128)(2,1)} %convolution_convert_fusion.5), channel_id=1, source_target_pairs={{0,8},{24,16},{1,9},{25,17},{2,10},{26,18},{3,11},{27,19},{4,12},{... | collective-permute-start | bytes 8650760 | tf_op jit(solution)/shard_map/ppermute | solution.py:633
  395.0 4.2 convolution_convert_fusion.2
  399.3 55.3 %collective-permute-done.70 = bf16[704,2048]{1,0:T(8,128)(2,1)} collective-permute-done((bf16[704,2048]{1,0:T(8,128)(2,1)}, bf16[704,2048]{1,0:T(8,128)(2,1)}, u32[]{:S(2)}, u32[]{:S(2)}) %collective-permute-start.70) | collective-permute-done | bytes 2883616 | tf_op jit(solution)/shard_map/ppermute | solution.py:633
  454.7 6.4 add_convert_fusion.5
  463.4 4.5 convolution_convert_fusion.6
  467.9 5.6 collective-permute-start.69
  477.2 5.7 add_convert_fusion.4
  482.9 49.4 %collective-permute-done.69 = bf16[704,2048]{1,0:T(8,128)(2,1)} collective-permute-done((bf16[704,2048]{1,0:T(8,128)(2,1)}, bf16[704,2048]{1,0:T(8,128)(2,1)}, u32[]{:S(2)}, u32[]{:S(2)}) %collective-permute-start.69) | collective-permute-done | bytes 2883616 | tf_op jit(solution)/shard_map/ppermute | solution.py:633
  532.3 5.7 add_convert_fusion.3
  540.3 4.8 convolution_convert_fusion.7
  545.1 7.3 collective-permute-start.68
  552.4 5.9 convolution_convert_fusion.1
  561.3 4.3 add_convert_fusion.2
  565.6 44.2 %collective-permute-done.68 = bf16[704,2048]{1,0:T(8,128)(2,1)} collective-permute-done((bf16[704,2048]{1,0:T(8,128)(2,1)}, bf16[704,2048]{1,0:T(8,128)(2,1)}, u32[]{:S(2)}, u32[]{:S(2)}) %collective-permute-start.68) | collective-permute-done | bytes 2883616 | tf_op jit(solution)/shard_map/ppermute | solution.py:633
  609.7 3.9 add_convert_fusion.1
  619.2 11.3 collective-permute-done.42
  638.3 6.9 collective-permute-done.43
  648.6 51.0 %collective-permute-done.93 = bf16[704,2048]{1,0:T(8,128)(2,1)S(1)} collective-permute-done((bf16[704,2048]{1,0:T(8,128)(2,1)S(1)}, bf16[704,2048]{1,0:T(8,128)(2,1)S(1)}, u32[]{:S(2)}, u32[]{:S(2)}) %collective-permute-start.93) | collective-permute-done | bytes 2883616 | tf_op jit(solution)/shard_map/ppermute | solution.py:640
  700.0 61.5 %collective-permute-done.91 = bf16[704,2048]{1,0:T(8,128)(2,1)S(1)} collective-permute-done((bf16[704,2048]{1,0:T(8,128)(2,1)S(1)}, bf16[704,2048]{1,0:T(8,128)(2,1)S(1)}, u32[]{:S(2)}, u32[]{:S(2)}) %collective-permute-start.91) | collective-permute-done | bytes 2883616 | tf_op jit(solution)/shard_map/ppermute | solution.py:640
  761.8 58.6 %collective-permute-done.92 = bf16[704,2048]{1,0:T(8,128)(2,1)S(1)} collective-permute-done((bf16[704,2048]{1,0:T(8,128)(2,1)S(1)}, bf16[704,2048]{1,0:T(8,128)(2,1)S(1)}, u32[]{:S(2)}, u32[]{:S(2)}) %collective-permute-start.92) | collective-permute-done | bytes 2883616 | tf_op jit(solution)/shard_map/ppermute | solution.py:640
  824.9 6.8 convert_bitcast_fusion
  831.7 5.6 collective-permute-done.46
  837.3 30.9 %collective-permute-done.47 = bf16[128,2176]{1,0:T(8,128)(2,1)S(1)} collective-permute-done((bf16[128,2176]{1,0:T(8,128)(2,1)S(1)}, bf16[128,2176]{1,0:T(8,128)(2,1)S(1)}, u32[]{:S(2)}, u32[]{:S(2)}) %collective-permute-start.47) | collective-permute-done | bytes 557088 | tf_op jit(solution)/shard_map/ppermute | solution.py:603
  878.6 5.8 convolution_convert_fusion
  897.2 4.6 collective-permute-done.90
  921.0 4.6 convolution_convert_fusion.10
  925.5 12.7 %collective-permute-start.67 = (bf16[256,2048]{1,0:T(8,128)(2,1)}, bf16[256,2048]{1,0:T(8,128)(2,1)}, u32[]{:S(2)}, u32[]{:S(2)}) collective-permute-start(bf16[256,2048]{1,0:T(8,128)(2,1)} %convolution_convert_fusion.10), channel_id=1, source_target_pairs={{0,8},{24,16},{1,9},{25,17},{2,10},{26,18},{3,11},{27,19},{4,12},{... | collective-permute-start | bytes 3145736 | tf_op jit(solution)/shard_map/ppermute | solution.py:633
  940.4 10.0 attend_backward.1.d_ref
  950.3 7.4 input_grad.1
  964.4 7.2 collective-permute-start.66
  977.2 17.9 %collective-permute-done.66 = bf16[2048,256]{1,0:T(8,128)(2,1)S(1)} collective-permute-done((bf16[2048,256]{1,0:T(8,128)(2,1)S(1)}, bf16[2048,256]{1,0:T(8,128)(2,1)S(1)}, u32[]{:S(2)}, u32[]{:S(2)}) %collective-permute-start.66) | collective-permute-done | bytes 1048608 | tf_op jit(solution)/shard_map/ppermute | solution.py:633
  999.3 6.9 collective-permute-done.57
  1012.1 4.3 collective-permute-done.58
  1020.3 8.6 collective-permute-start.83
  1036.6 17.3 %collective-permute-done.84 = f32[3,256]{1,0:T(4,128)S(1)} collective-permute-done((f32[3,256]{1,0:T(4,128)S(1)}, f32[3,256]{1,0:T(4,128)S(1)}, u32[]{:S(2)}, u32[]{:S(2)}) %collective-permute-start.84) | collective-permute-done | bytes 3104 | tf_op jit(solution)/shard_map/ppermute | solution.py:539
  1058.1 10.4 collective-permute-done.64
  1080.1 13.0 %collective-permute-done.25 = bf16[128,2048]{1,0:T(8,128)(2,1)} collective-permute-done((bf16[128,2048]{1,0:T(8,128)(2,1)}, bf16[128,2048]{1,0:T(8,128)(2,1)}, u32[]{:S(2)}, u32[]{:S(2)}) %collective-permute-start.25) | collective-permute-done | bytes 524320 | tf_op jit(solution)/shard_map/ppermute | solution.py:603
  1093.1 4.0 fusion.24
  1099.0 15.3 %collective-permute-done.85 = bf16[256,2048]{1,0:T(8,128)(2,1)} collective-permute-done((bf16[256,2048]{1,0:T(8,128)(2,1)}, bf16[256,2048]{1,0:T(8,128)(2,1)}, u32[]{:S(2)}, u32[]{:S(2)}) %collective-permute-start.85) | collective-permute-done | bytes 1048608 | tf_op jit(solution)/shard_map/ppermute | solution.py:640
  1121.4 15.3 %collective-permute-done.76 = bf16[2048,256]{1,0:T(8,128)(2,1)S(1)} collective-permute-done((bf16[2048,256]{1,0:T(8,128)(2,1)S(1)}, bf16[2048,256]{1,0:T(8,128)(2,1)S(1)}, u32[]{:S(2)}, u32[]{:S(2)}) %collective-permute-start.76) | collective-permute-done | bytes 1048608 | tf_op jit(solution)/shard_map/ppermute | solution.py:640
  1137.7 21.4 %collective-permute-done.79 = bf16[2048,256]{1,0:T(8,128)(2,1)S(1)} collective-permute-done((bf16[2048,256]{1,0:T(8,128)(2,1)S(1)}, bf16[2048,256]{1,0:T(8,128)(2,1)S(1)}, u32[]{:S(2)}, u32[]{:S(2)}) %collective-permute-start.79) | collective-permute-done | bytes 1048608 | tf_op jit(solution)/shard_map/ppermute | solution.py:640
  1161.8 3.8 copy.126
  1165.6 16.1 %collective-permute-done.82 = bf16[2048,256]{1,0:T(8,128)(2,1)} collective-permute-done((bf16[2048,256]{1,0:T(8,128)(2,1)S(1)}, bf16[2048,256]{1,0:T(8,128)(2,1)}, u32[]{:S(2)}, u32[]{:S(2)}) %collective-permute-start.82) | collective-permute-done | bytes 1048608 | tf_op jit(solution)/shard_map/ppermute | solution.py:640
  1188.3 7.0 copy.125
  (457 shorter events, 239.7 us)
Async XLA Ops:
  7.2 319.9 %all-gather.7.cloned.1.call-start = ((), (), s32[]{:S(2)}) async-start(), calls=%async_computation.11 | async-start | bytes 12976128 | tf_op jit(solution)/shard_map/all_gather | solution.py:687
  20.9 306.2 %all-gather.5.cloned.1.call-start = ((), (), s32[]{:S(2)}) async-start(), calls=%async_computation.10 | async-start | bytes 25952256 | tf_op jit(solution)/shard_map/all_gather | solution.py:686
  24.7 1055.3 %reduce-scatter.6.cloned.1.call-start = ((), (), s32[]{:S(2)}) async-start(), calls=%async_computation.5 | async-start | bytes 4718592 | tf_op jit(solution)/shard_map/reduce_scatter | solution.py:741
  24.8 16.9 %collective-permute-start = (bf16[128,2048]{1,0:T(8,128)(2,1)S(1)}, bf16[128,2048]{1,0:T(8,128)(2,1)}, u32[]{:S(2)}, u32[]{:S(2)}) collective-permute-start(bf16[128,2048]{1,0:T(8,128)(2,1)S(1)} %copy-done.1), channel_id=1, source_target_pairs={{0,1},{1,0},{2,3},{3,2},{4,5},{5,4},{6,7},{7,6},{8,9},{9,8},{10,11... | collective-permute-start | bytes 1572872 | tf_op jit(solution)/shard_map/ppermute | solution.py:539
  39.0 21.3 %collective-permute-start.3 = (bf16[128,2048]{1,0:T(8,128)(2,1)S(1)}, bf16[128,2048]{1,0:T(8,128)(2,1)S(1)}, u32[]{:S(2)}, u32[]{:S(2)}) collective-permute-start(bf16[128,2048]{1,0:T(8,128)(2,1)S(1)} %get-tuple-element.166), channel_id=1, source_target_pairs={{0,2},{1,3},{2,0},{3,1},{4,6},{5,7},{6,4},{7,5},{8,10},{9,11},{10,... | collective-permute-start | bytes 1572872 | tf_op jit(solution)/shard_map/ppermute | solution.py:539
  40.6 20.7 %collective-permute-start.5 = (bf16[128,2048]{1,0:T(8,128)(2,1)S(1)}, bf16[128,2048]{1,0:T(8,128)(2,1)S(1)}, u32[]{:S(2)}, u32[]{:S(2)}) collective-permute-start(bf16[128,2048]{1,0:T(8,128)(2,1)S(1)} %get-tuple-element.164), channel_id=1, source_target_pairs={{0,4},{1,5},{2,6},{3,7},{4,0},{5,1},{6,2},{7,3},{8,12},{9,13},{10,... | collective-permute-start | bytes 1572872 | tf_op jit(solution)/shard_map/ppermute | solution.py:539
  41.7 21.3 %collective-permute-start.4 = (bf16[128,2048]{1,0:T(8,128)(2,1)S(1)}, bf16[128,2048]{1,0:T(8,128)(2,1)S(1)}, u32[]{:S(2)}, u32[]{:S(2)}) collective-permute-start(bf16[128,2048]{1,0:T(8,128)(2,1)S(1)} %get-tuple-element.165), channel_id=1, source_target_pairs={{0,1},{1,0},{2,3},{3,2},{4,5},{5,4},{6,7},{7,6},{8,9},{9,8},{10,11... | collective-permute-start | bytes 1572872 | tf_op jit(solution)/shard_map/ppermute | solution.py:539
  70.7 25.1 %collective-permute-start.34 = (bf16[128,2048]{1,0:T(8,128)(2,1)S(1)}, bf16[128,2048]{1,0:T(8,128)(2,1)}, u32[]{:S(2)}, u32[]{:S(2)}) collective-permute-start(bf16[128,2048]{1,0:T(8,128)(2,1)S(1)} %copy-done.3), channel_id=1, source_target_pairs={{0,1},{1,0},{2,3},{3,2},{4,5},{5,4},{6,7},{7,6},{8,9},{9,8},{10,11... | collective-permute-start | bytes 1572872 | tf_op jit(solution)/shard_map/ppermute | solution.py:539
  70.8 22.7 %collective-permute-start.35 = (bf16[64,2048]{1,0:T(8,128)(2,1)S(1)}, bf16[64,2048]{1,0:T(8,128)(2,1)S(1)}, u32[]{:S(2)}, u32[]{:S(2)}) collective-permute-start(bf16[64,2048]{1,0:T(8,128)(2,1)S(1)} %get-tuple-element.150), channel_id=1, source_target_pairs={{0,2},{1,3},{2,0},{3,1},{4,6},{5,7},{6,4},{7,5},{8,10},{9,11},{10,... | collective-permute-start | bytes 786440 | tf_op jit(solution)/shard_map/ppermute | solution.py:539
  72.5 21.0 %collective-permute-start.36 = (bf16[64,2048]{1,0:T(8,128)(2,1)S(1)}, bf16[64,2048]{1,0:T(8,128)(2,1)S(1)}, u32[]{:S(2)}, u32[]{:S(2)}) collective-permute-start(bf16[64,2048]{1,0:T(8,128)(2,1)S(1)} %get-tuple-element.149), channel_id=1, source_target_pairs={{0,4},{1,5},{2,6},{3,7},{4,0},{5,1},{6,2},{7,3},{8,12},{9,13},{10,... | collective-permute-start | bytes 786440 | tf_op jit(solution)/shard_map/ppermute | solution.py:539
  93.7 23.2 %collective-permute-start.37 = (bf16[128,2048]{1,0:T(8,128)(2,1)S(1)}, bf16[128,2048]{1,0:T(8,128)(2,1)S(1)}, u32[]{:S(2)}, u32[]{:S(2)}) collective-permute-start(bf16[128,2048]{1,0:T(8,128)(2,1)S(1)} %get-tuple-element.160), channel_id=1, source_target_pairs={{0,2},{1,3},{2,0},{3,1},{4,6},{5,7},{6,4},{7,5},{8,10},{9,11},{10,... | collective-permute-start | bytes 1572872 | tf_op jit(solution)/shard_map/ppermute | solution.py:539
  94.3 22.6 %collective-permute-start.39 = (bf16[128,2048]{1,0:T(8,128)(2,1)S(1)}, bf16[128,2048]{1,0:T(8,128)(2,1)S(1)}, u32[]{:S(2)}, u32[]{:S(2)}) collective-permute-start(bf16[128,2048]{1,0:T(8,128)(2,1)S(1)} %get-tuple-element.158), channel_id=1, source_target_pairs={{0,4},{1,5},{2,6},{3,7},{4,0},{5,1},{6,2},{7,3},{8,12},{9,13},{10,... | collective-permute-start | bytes 1572872 | tf_op jit(solution)/shard_map/ppermute | solution.py:539
  95.0 24.9 %collective-permute-start.10 = (bf16[2,2,128,2048]{3,2,1,0:T(8,128)(2,1)S(1)}, bf16[2,2,128,2048]{3,2,1,0:T(8,128)(2,1)S(1)}, u32[]{:S(2)}, u32[]{:S(2)}) collective-permute-start(bf16[2,2,128,2048]{3,2,1,0:T(8,128)(2,1)S(1)} %slice_bitcast_fusion.4), channel_id=1, source_target_pairs={{0,1},{1,0},{2,3},{3,2},{4,5},{5,4},{6,7},{7,6},{8,9},{9,8},{10,11... | collective-permute-start | bytes 6291464 | tf_op jit(solution)/shard_map/ppermute | solution.py:539
  95.2 22.0 %collective-permute-start.38 = (bf16[128,2048]{1,0:T(8,128)(2,1)S(1)}, bf16[128,2048]{1,0:T(8,128)(2,1)S(1)}, u32[]{:S(2)}, u32[]{:S(2)}) collective-permute-start(bf16[128,2048]{1,0:T(8,128)(2,1)S(1)} %get-tuple-element.159), channel_id=1, source_target_pairs={{0,1},{1,0},{2,3},{3,2},{4,5},{5,4},{6,7},{7,6},{8,9},{9,8},{10,11... | collective-permute-start | bytes 1572872 | tf_op jit(solution)/shard_map/ppermute | solution.py:539
  120.9 17.0 %collective-permute-start.11 = (bf16[2,64,2048]{2,1,0:T(8,128)(2,1)S(1)}, bf16[2,64,2048]{2,1,0:T(8,128)(2,1)S(1)}, u32[]{:S(2)}, u32[]{:S(2)}) collective-permute-start(bf16[2,64,2048]{2,1,0:T(8,128)(2,1)S(1)} %slice_bitcast_fusion.25), channel_id=1, source_target_pairs={{0,2},{1,3},{2,0},{3,1},{4,6},{5,7},{6,4},{7,5},{8,10},{9,11},{10,... | collective-permute-start | bytes 1572872 | tf_op jit(solution)/shard_map/ppermute | solution.py:539
  122.4 17.8 %collective-permute-start.13 = (bf16[2,64,2048]{2,1,0:T(8,128)(2,1)S(1)}, bf16[2,64,2048]{2,1,0:T(8,128)(2,1)S(1)}, u32[]{:S(2)}, u32[]{:S(2)}) collective-permute-start(bf16[2,64,2048]{2,1,0:T(8,128)(2,1)S(1)} %slice_bitcast_fusion.23), channel_id=1, source_target_pairs={{0,4},{1,5},{2,6},{3,7},{4,0},{5,1},{6,2},{7,3},{8,12},{9,13},{10,... | collective-permute-start | bytes 1572872 | tf_op jit(solution)/shard_map/ppermute | solution.py:539
  171.0 17.3 %collective-permute-start.30 = (bf16[128,2048]{1,0:T(8,128)(2,1)S(1)}, bf16[128,2048]{1,0:T(8,128)(2,1)S(1)}, u32[]{:S(2)}, u32[]{:S(2)}) collective-permute-start(bf16[128,2048]{1,0:T(8,128)(2,1)S(1)} %get-tuple-element.163), channel_id=1, source_target_pairs={{0,2},{1,3},{2,0},{3,1},{4,6},{5,7},{6,4},{7,5},{8,10},{9,11},{10,... | collective-permute-start | bytes 1572872 | tf_op jit(solution)/shard_map/ppermute | solution.py:539
  171.7 17.9 %collective-permute-start.32 = (bf16[128,2048]{1,0:T(8,128)(2,1)S(1)}, bf16[128,2048]{1,0:T(8,128)(2,1)S(1)}, u32[]{:S(2)}, u32[]{:S(2)}) collective-permute-start(bf16[128,2048]{1,0:T(8,128)(2,1)S(1)} %get-tuple-element.161), channel_id=1, source_target_pairs={{0,4},{1,5},{2,6},{3,7},{4,0},{5,1},{6,2},{7,3},{8,12},{9,13},{10,... | collective-permute-start | bytes 1572872 | tf_op jit(solution)/shard_map/ppermute | solution.py:539
  172.7 17.1 %collective-permute-start.31 = (bf16[128,2048]{1,0:T(8,128)(2,1)S(1)}, bf16[128,2048]{1,0:T(8,128)(2,1)S(1)}, u32[]{:S(2)}, u32[]{:S(2)}) collective-permute-start(bf16[128,2048]{1,0:T(8,128)(2,1)S(1)} %get-tuple-element.162), channel_id=1, source_target_pairs={{0,1},{1,0},{2,3},{3,2},{4,5},{5,4},{6,7},{7,6},{8,9},{9,8},{10,11... | collective-permute-start | bytes 1572872 | tf_op jit(solution)/shard_map/ppermute | solution.py:539
  236.1 924.1 %reduce-scatter.12.cloned.1.call-start = ((), (), s32[]{:S(2)}) async-start(), calls=%async_computation.8 | async-start | bytes 6488064 | tf_op jit(solution)/shard_map/reduce_scatter | solution.py:796
  236.2 54.3 %collective-permute-start.21 = (bf16[128,2048]{1,0:T(8,128)(2,1)S(1)}, bf16[128,2048]{1,0:T(8,128)(2,1)}, u32[]{:S(2)}, u32[]{:S(2)}) collective-permute-start(bf16[128,2048]{1,0:T(8,128)(2,1)S(1)} %copy-done.3), channel_id=1, source_target_pairs={{0,8},{8,16},{16,24},{24,0},{1,9},{9,17},{17,25},{25,1},{2,10},{10... | collective-permute-start | bytes 1572872 | tf_op jit(solution)/shard_map/ppermute | solution.py:603
  238.0 54.6 %collective-permute-start.22 = (bf16[128,2048]{1,0:T(8,128)(2,1)S(1)}, bf16[128,2048]{1,0:T(8,128)(2,1)}, u32[]{:S(2)}, u32[]{:S(2)}) collective-permute-start(bf16[128,2048]{1,0:T(8,128)(2,1)S(1)} %copy-done.3), channel_id=1, source_target_pairs={{0,16},{8,24},{16,0},{24,8},{1,17},{9,25},{17,1},{25,9},{2,18},{10... | collective-permute-start | bytes 1572872 | tf_op jit(solution)/shard_map/ppermute | solution.py:603
  240.4 52.2 %collective-permute-start.23 = (bf16[128,2048]{1,0:T(8,128)(2,1)S(1)}, bf16[128,2048]{1,0:T(8,128)(2,1)}, u32[]{:S(2)}, u32[]{:S(2)}) collective-permute-start(bf16[128,2048]{1,0:T(8,128)(2,1)S(1)} %copy-done.3), channel_id=1, source_target_pairs={{0,24},{8,0},{16,8},{24,16},{1,25},{9,1},{17,9},{25,17},{2,26},{10... | collective-permute-start | bytes 1572872 | tf_op jit(solution)/shard_map/ppermute | solution.py:603
  242.6 32.2 %collective-permute-start.15 = (s32[8,128]{1,0:T(8,128)S(1)}, s32[8,128]{1,0:T(8,128)S(1)}, u32[]{:S(2)}, u32[]{:S(2)}) collective-permute-start(s32[8,128]{1,0:T(8,128)S(1)} %get-tuple-element.175), channel_id=1, source_target_pairs={{0,8},{8,16},{16,24},{24,0},{1,9},{9,17},{17,25},{25,1},{2,10},{10... | collective-permute-start | bytes 12296 | tf_op jit(solution)/shard_map/ppermute | solution.py:603
  243.3 42.8 %collective-permute-start.16 = (s32[8,128]{1,0:T(8,128)S(1)}, s32[8,128]{1,0:T(8,128)S(1)}, u32[]{:S(2)}, u32[]{:S(2)}) collective-permute-start(s32[8,128]{1,0:T(8,128)S(1)} %get-tuple-element.175), channel_id=1, source_target_pairs={{0,16},{8,24},{16,0},{24,8},{1,17},{9,25},{17,1},{25,9},{2,18},{10... | collective-permute-start | bytes 12296 | tf_op jit(solution)/shard_map/ppermute | solution.py:603
  286.0 16.8 %collective-permute-start.18 = (bf16[128,2048]{1,0:T(8,128)(2,1)S(1)}, bf16[128,2048]{1,0:T(8,128)(2,1)}, u32[]{:S(2)}, u32[]{:S(2)}) collective-permute-start(bf16[128,2048]{1,0:T(8,128)(2,1)S(1)} %get-tuple-element.129), channel_id=1, source_target_pairs={{0,8},{8,16},{16,24},{24,0},{1,9},{9,17},{17,25},{25,1},{2,10},{10... | collective-permute-start | bytes 1572872 | tf_op jit(solution)/shard_map/ppermute | solution.py:603
  286.5 37.6 %collective-permute-start.19 = (bf16[128,2048]{1,0:T(8,128)(2,1)S(1)}, bf16[128,2048]{1,0:T(8,128)(2,1)}, u32[]{:S(2)}, u32[]{:S(2)}) collective-permute-start(bf16[128,2048]{1,0:T(8,128)(2,1)S(1)} %get-tuple-element.129), channel_id=1, source_target_pairs={{0,16},{8,24},{16,0},{24,8},{1,17},{9,25},{17,1},{25,9},{2,18},{10... | collective-permute-start | bytes 1572872 | tf_op jit(solution)/shard_map/ppermute | solution.py:603
  290.5 33.7 %collective-permute-start.20 = (bf16[128,2048]{1,0:T(8,128)(2,1)S(1)}, bf16[128,2048]{1,0:T(8,128)(2,1)}, u32[]{:S(2)}, u32[]{:S(2)}) collective-permute-start(bf16[128,2048]{1,0:T(8,128)(2,1)S(1)} %get-tuple-element.129), channel_id=1, source_target_pairs={{0,24},{8,0},{16,8},{24,16},{1,25},{9,1},{17,9},{25,17},{2,26},{10... | collective-permute-start | bytes 1572872 | tf_op jit(solution)/shard_map/ppermute | solution.py:603
  373.2 787.0 %reduce-scatter.14.cloned.1.call-start = ((), (), s32[]{:S(2)}) async-start(), calls=%async_computation.9 | async-start | bytes 6488064 | tf_op jit(solution)/shard_map/reduce_scatter | solution.py:796
  380.7 73.9 %collective-permute-start.70 = (bf16[704,2048]{1,0:T(8,128)(2,1)}, bf16[704,2048]{1,0:T(8,128)(2,1)}, u32[]{:S(2)}, u32[]{:S(2)}) collective-permute-start(bf16[704,2048]{1,0:T(8,128)(2,1)} %convolution_convert_fusion.5), channel_id=1, source_target_pairs={{0,8},{24,16},{1,9},{25,17},{2,10},{26,18},{3,11},{27,19},{4,12},{... | collective-permute-start | bytes 8650760 | tf_op jit(solution)/shard_map/ppermute | solution.py:633
  399.3 786.9 %reduce-scatter.8.cloned.1.call-start = ((), (), s32[]{:S(2)}) async-start(), calls=%async_computation.6 | async-start | bytes 12976128 | tf_op jit(solution)/shard_map/reduce_scatter | solution.py:793
  461.1 16.1 %collective-permute-start.71 = (bf16[704,2048]{1,0:T(8,128)(2,1)}, bf16[704,2048]{1,0:T(8,128)(2,1)}, u32[]{:S(2)}, u32[]{:S(2)}) collective-permute-start(bf16[704,2048]{1,0:T(8,128)(2,1)} %add_convert_fusion.5), channel_id=1, source_target_pairs={{8,16},{16,8},{9,17},{17,9},{10,18},{18,10},{11,19},{19,11},{12,20... | collective-permute-start | bytes 8650760 | tf_op jit(solution)/shard_map/ppermute | solution.py:637
  467.9 64.4 %collective-permute-start.69 = (bf16[704,2048]{1,0:T(8,128)(2,1)}, bf16[704,2048]{1,0:T(8,128)(2,1)}, u32[]{:S(2)}, u32[]{:S(2)}) collective-permute-start(bf16[704,2048]{1,0:T(8,128)(2,1)} %convolution_convert_fusion.6), channel_id=1, source_target_pairs={{0,8},{24,16},{1,9},{25,17},{2,10},{26,18},{3,11},{27,19},{4,12},{... | collective-permute-start | bytes 8650760 | tf_op jit(solution)/shard_map/ppermute | solution.py:633
  477.2 81.2 %collective-permute-start.41 = (bf16[2,2,128,2176]{3,2,1,0:T(8,128)(2,1)}, bf16[2,2,128,2176]{3,2,1,0:T(8,128)(2,1)}, u32[]{:S(2)}, u32[]{:S(2)}) collective-permute-start(bf16[2,2,128,2176]{3,2,1,0:T(8,128)(2,1)} %slice_bitcast_fusion), channel_id=1, source_target_pairs={{0,1},{1,0},{2,3},{3,2},{4,5},{5,4},{6,7},{7,6},{8,9},{9,8},{10,11... | collective-permute-start | bytes 6684680 | tf_op jit(solution)/shard_map/ppermute | solution.py:539
  538.0 23.3 %collective-permute-start.72 = (bf16[704,2048]{1,0:T(8,128)(2,1)}, bf16[704,2048]{1,0:T(8,128)(2,1)}, u32[]{:S(2)}, u32[]{:S(2)}) collective-permute-start(bf16[704,2048]{1,0:T(8,128)(2,1)} %add_convert_fusion.3), channel_id=1, source_target_pairs={{8,16},{16,8},{9,17},{17,9},{10,18},{18,10},{11,19},{19,11},{12,20... | collective-permute-start | bytes 8650760 | tf_op jit(solution)/shard_map/ppermute | solution.py:637
  545.1 64.7 %collective-permute-start.68 = (bf16[704,2048]{1,0:T(8,128)(2,1)}, bf16[704,2048]{1,0:T(8,128)(2,1)}, u32[]{:S(2)}, u32[]{:S(2)}) collective-permute-start(bf16[704,2048]{1,0:T(8,128)(2,1)} %convolution_convert_fusion.7), channel_id=1, source_target_pairs={{0,8},{24,16},{1,9},{25,17},{2,10},{26,18},{3,11},{27,19},{4,12},{... | collective-permute-start | bytes 8650760 | tf_op jit(solution)/shard_map/ppermute | solution.py:633
  558.3 627.9 %reduce-scatter.10.cloned.1.call-start = ((), (), s32[]{:S(2)}) async-start(), calls=%async_computation.7 | async-start | bytes 12976128 | tf_op jit(solution)/shard_map/reduce_scatter | solution.py:793
  613.6 22.0 %collective-permute-start.73 = (bf16[704,2048]{1,0:T(8,128)(2,1)S(1)}, bf16[704,2048]{1,0:T(8,128)(2,1)S(1)}, u32[]{:S(2)}, u32[]{:S(2)}) collective-permute-start(bf16[704,2048]{1,0:T(8,128)(2,1)S(1)} %add_convert_fusion.1), channel_id=1, source_target_pairs={{8,16},{16,8},{9,17},{17,9},{10,18},{18,10},{11,19},{19,11},{12,20... | collective-permute-start | bytes 8650760 | tf_op jit(solution)/shard_map/ppermute | solution.py:637
  614.6 15.9 %collective-permute-start.42 = (bf16[2,64,2176]{2,1,0:T(8,128)(2,1)S(1)}, bf16[2,64,2176]{2,1,0:T(8,128)(2,1)S(1)}, u32[]{:S(2)}, u32[]{:S(2)}) collective-permute-start(bf16[2,64,2176]{2,1,0:T(8,128)(2,1)S(1)} %slice_bitcast_fusion.8), channel_id=1, source_target_pairs={{0,2},{1,3},{2,0},{3,1},{4,6},{5,7},{6,4},{7,5},{8,10},{9,11},{10,... | collective-permute-start | bytes 1671176 | tf_op jit(solution)/shard_map/ppermute | solution.py:539
  632.4 67.3 %collective-permute-start.93 = (bf16[704,2048]{1,0:T(8,128)(2,1)S(1)}, bf16[704,2048]{1,0:T(8,128)(2,1)S(1)}, u32[]{:S(2)}, u32[]{:S(2)}) collective-permute-start(bf16[704,2048]{1,0:T(8,128)(2,1)S(1)} %copy-done.4), channel_id=1, source_target_pairs={{8,0},{16,24},{9,1},{17,25},{10,2},{18,26},{11,3},{19,27},{12,4},{... | collective-permute-start | bytes 8650760 | tf_op jit(solution)/shard_map/ppermute | solution.py:640
  634.3 127.2 %collective-permute-start.91 = (bf16[704,2048]{1,0:T(8,128)(2,1)S(1)}, bf16[704,2048]{1,0:T(8,128)(2,1)S(1)}, u32[]{:S(2)}, u32[]{:S(2)}) collective-permute-start(bf16[704,2048]{1,0:T(8,128)(2,1)S(1)} %add_convert_fusion.2), channel_id=1, source_target_pairs={{8,0},{16,24},{9,1},{17,25},{10,2},{18,26},{11,3},{19,27},{12,4},{... | collective-permute-start | bytes 8650760 | tf_op jit(solution)/shard_map/ppermute | solution.py:640
  637.0 183.3 %collective-permute-start.92 = (bf16[704,2048]{1,0:T(8,128)(2,1)S(1)}, bf16[704,2048]{1,0:T(8,128)(2,1)S(1)}, u32[]{:S(2)}, u32[]{:S(2)}) collective-permute-start(bf16[704,2048]{1,0:T(8,128)(2,1)S(1)} %add_convert_fusion), channel_id=1, source_target_pairs={{8,0},{16,24},{9,1},{17,25},{10,2},{18,26},{11,3},{19,27},{12,4},{... | collective-permute-start | bytes 8650760 | tf_op jit(solution)/shard_map/ppermute | solution.py:640
  820.8 16.5 %collective-permute-start.46 = (bf16[128,2176]{1,0:T(8,128)(2,1)S(1)}, bf16[128,2176]{1,0:T(8,128)(2,1)S(1)}, u32[]{:S(2)}, u32[]{:S(2)}) collective-permute-start(bf16[128,2176]{1,0:T(8,128)(2,1)S(1)} %get-tuple-element.132), channel_id=1, source_target_pairs={{0,24},{8,0},{16,8},{24,16},{1,25},{9,1},{17,9},{25,17},{2,26},{10... | collective-permute-start | bytes 1671176 | tf_op jit(solution)/shard_map/ppermute | solution.py:603
  824.3 44.0 %collective-permute-start.47 = (bf16[128,2176]{1,0:T(8,128)(2,1)S(1)}, bf16[128,2176]{1,0:T(8,128)(2,1)S(1)}, u32[]{:S(2)}, u32[]{:S(2)}) collective-permute-start(bf16[128,2176]{1,0:T(8,128)(2,1)S(1)} %get-tuple-element.134), channel_id=1, source_target_pairs={{0,16},{8,24},{16,0},{24,8},{1,17},{9,25},{17,1},{25,9},{2,18},{10... | collective-permute-start | bytes 1671176 | tf_op jit(solution)/shard_map/ppermute | solution.py:603
  824.3 44.0 %collective-permute-start.48 = (bf16[128,2176]{1,0:T(8,128)(2,1)S(1)}, bf16[128,2176]{1,0:T(8,128)(2,1)S(1)}, u32[]{:S(2)}, u32[]{:S(2)}) collective-permute-start(bf16[128,2176]{1,0:T(8,128)(2,1)S(1)} %get-tuple-element.133), channel_id=1, source_target_pairs={{0,8},{8,16},{16,24},{24,0},{1,9},{9,17},{17,25},{25,1},{2,10},{10... | collective-permute-start | bytes 1671176 | tf_op jit(solution)/shard_map/ppermute | solution.py:603
  884.4 18.1 %collective-permute-start.49 = (bf16[128,2048]{1,0:T(8,128)(2,1)S(1)}, bf16[128,2048]{1,0:T(8,128)(2,1)}, u32[]{:S(2)}, u32[]{:S(2)}) collective-permute-start(bf16[128,2048]{1,0:T(8,128)(2,1)S(1)} %get-tuple-element.127), channel_id=1, source_target_pairs={{0,1},{1,0},{2,3},{3,2},{4,5},{5,4},{6,7},{7,6},{8,9},{9,8},{10,11... | collective-permute-start | bytes 1572872 | tf_op jit(solution)/shard_map/ppermute | solution.py:539
  896.4 182.0 %collective-permute-start.24 = (bf16[128,2048]{1,0:T(8,128)(2,1)}, bf16[128,2048]{1,0:T(8,128)(2,1)}, u32[]{:S(2)}, u32[]{:S(2)}) collective-permute-start(bf16[128,2048]{1,0:T(8,128)(2,1)} %get-tuple-element.139), channel_id=1, source_target_pairs={{0,24},{8,0},{16,8},{24,16},{1,25},{9,1},{17,9},{25,17},{2,26},{10... | collective-permute-start | bytes 1572872 | tf_op jit(solution)/shard_map/ppermute | solution.py:603
  925.5 34.9 %collective-permute-start.67 = (bf16[256,2048]{1,0:T(8,128)(2,1)}, bf16[256,2048]{1,0:T(8,128)(2,1)}, u32[]{:S(2)}, u32[]{:S(2)}) collective-permute-start(bf16[256,2048]{1,0:T(8,128)(2,1)} %convolution_convert_fusion.10), channel_id=1, source_target_pairs={{0,8},{24,16},{1,9},{25,17},{2,10},{26,18},{3,11},{27,19},{4,12},{... | collective-permute-start | bytes 3145736 | tf_op jit(solution)/shard_map/ppermute | solution.py:633
  959.7 35.4 %collective-permute-start.56 = (bf16[2,2,128,2048]{3,2,1,0:T(8,128)(2,1)S(1)}, bf16[2,2,128,2048]{3,2,1,0:T(8,128)(2,1)S(1)}, u32[]{:S(2)}, u32[]{:S(2)}) collective-permute-start(bf16[2,2,128,2048]{3,2,1,0:T(8,128)(2,1)S(1)} %slice_bitcast_fusion.2), channel_id=1, source_target_pairs={{0,1},{1,0},{2,3},{3,2},{4,5},{5,4},{6,7},{7,6},{8,9},{9,8},{10,11... | collective-permute-start | bytes 6291464 | tf_op jit(solution)/shard_map/ppermute | solution.py:539
  964.4 30.7 %collective-permute-start.66 = (bf16[2048,256]{1,0:T(8,128)(2,1)S(1)}, bf16[2048,256]{1,0:T(8,128)(2,1)S(1)}, u32[]{:S(2)}, u32[]{:S(2)}) collective-permute-start(bf16[2048,256]{1,0:T(8,128)(2,1)S(1)} %convolution_convert_fusion.11), channel_id=1, source_target_pairs={{0,8},{24,16},{1,9},{25,17},{2,10},{26,18},{3,11},{27,19},{4,12},{... | collective-permute-start | bytes 3145736 | tf_op jit(solution)/shard_map/ppermute | solution.py:633
  972.9 45.4 %collective-permute-start.77 = (bf16[2048,256]{1,0:T(8,128)(2,1)S(1)}, bf16[2048,256]{1,0:T(8,128)(2,1)S(1)}, u32[]{:S(2)}, u32[]{:S(2)}) collective-permute-start(bf16[2048,256]{1,0:T(8,128)(2,1)S(1)} %convolution_convert_fusion.9), channel_id=1, source_target_pairs={{0,8},{24,16},{1,9},{25,17},{2,10},{26,18},{3,11},{27,19},{4,12},{... | collective-permute-start | bytes 3145736 | tf_op jit(solution)/shard_map/ppermute | solution.py:633
  998.6 18.4 %collective-permute-start.75 = (bf16[2048,256]{1,0:T(8,128)(2,1)S(1)}, bf16[2048,256]{1,0:T(8,128)(2,1)S(1)}, u32[]{:S(2)}, u32[]{:S(2)}) collective-permute-start(bf16[2048,256]{1,0:T(8,128)(2,1)S(1)} %add_convert_fusion.11), channel_id=1, source_target_pairs={{8,16},{16,8},{9,17},{17,9},{10,18},{18,10},{11,19},{19,11},{12,20... | collective-permute-start | bytes 3145736 | tf_op jit(solution)/shard_map/ppermute | solution.py:637
  1018.5 52.4 %collective-permute-start.78 = (bf16[2048,256]{1,0:T(8,128)(2,1)S(1)}, bf16[2048,256]{1,0:T(8,128)(2,1)S(1)}, u32[]{:S(2)}, u32[]{:S(2)}) collective-permute-start(bf16[2048,256]{1,0:T(8,128)(2,1)S(1)} %add_convert_fusion.9), channel_id=1, source_target_pairs={{8,16},{16,8},{9,17},{17,9},{10,18},{18,10},{11,19},{19,11},{12,20... | collective-permute-start | bytes 3145736 | tf_op jit(solution)/shard_map/ppermute | solution.py:637
  1028.8 44.8 %collective-permute-start.80 = (bf16[2048,256]{1,0:T(8,128)(2,1)S(1)}, bf16[2048,256]{1,0:T(8,128)(2,1)S(1)}, u32[]{:S(2)}, u32[]{:S(2)}) collective-permute-start(bf16[2048,256]{1,0:T(8,128)(2,1)S(1)} %convolution_convert_fusion.8), channel_id=1, source_target_pairs={{0,8},{24,16},{1,9},{25,17},{2,10},{26,18},{3,11},{27,19},{4,12},{... | collective-permute-start | bytes 3145736 | tf_op jit(solution)/shard_map/ppermute | solution.py:633
  1032.9 21.0 %collective-permute-start.84 = (f32[3,256]{1,0:T(4,128)S(1)}, f32[3,256]{1,0:T(4,128)S(1)}, u32[]{:S(2)}, u32[]{:S(2)}) collective-permute-start(f32[3,256]{1,0:T(4,128)S(1)} %add.360), channel_id=1, source_target_pairs={{0,16},{8,24},{16,0},{24,8},{1,17},{9,25},{17,1},{25,9},{2,18},{10... | collective-permute-start | bytes 9224 | tf_op jit(solution)/shard_map/ppermute | solution.py:539
  1034.6 23.3 %collective-permute-start.63 = (f32[1,2048]{1,0:T(1,128)S(1)}, f32[1,2048]{1,0:T(1,128)S(1)}, u32[]{:S(2)}, u32[]{:S(2)}) collective-permute-start(f32[1,2048]{1,0:T(1,128)S(1)} %add.341), channel_id=1, source_target_pairs={{0,4},{1,5},{2,6},{3,7},{4,0},{5,1},{6,2},{7,3},{8,12},{9,13},{10,... | collective-permute-start | bytes 24584 | tf_op jit(solution)/shard_map/ppermute | solution.py:539
  1053.9 39.2 %collective-permute-start.25 = (bf16[128,2048]{1,0:T(8,128)(2,1)}, bf16[128,2048]{1,0:T(8,128)(2,1)}, u32[]{:S(2)}, u32[]{:S(2)}) collective-permute-start(bf16[128,2048]{1,0:T(8,128)(2,1)} %get-tuple-element.141), channel_id=1, source_target_pairs={{0,16},{8,24},{16,0},{24,8},{1,17},{9,25},{17,1},{25,9},{2,18},{10... | collective-permute-start | bytes 1572872 | tf_op jit(solution)/shard_map/ppermute | solution.py:603
  1068.5 24.6 %collective-permute-start.26 = (bf16[128,2048]{1,0:T(8,128)(2,1)}, bf16[128,2048]{1,0:T(8,128)(2,1)}, u32[]{:S(2)}, u32[]{:S(2)}) collective-permute-start(bf16[128,2048]{1,0:T(8,128)(2,1)} %get-tuple-element.140), channel_id=1, source_target_pairs={{0,8},{8,16},{16,24},{24,0},{1,9},{9,17},{17,25},{25,1},{2,10},{10... | collective-permute-start | bytes 1572872 | tf_op jit(solution)/shard_map/ppermute | solution.py:603
  1071.0 43.3 %collective-permute-start.85 = (bf16[256,2048]{1,0:T(8,128)(2,1)}, bf16[256,2048]{1,0:T(8,128)(2,1)}, u32[]{:S(2)}, u32[]{:S(2)}) collective-permute-start(bf16[256,2048]{1,0:T(8,128)(2,1)} %add_convert_fusion.12), channel_id=1, source_target_pairs={{8,0},{16,24},{9,1},{17,25},{10,2},{18,26},{11,3},{19,27},{12,4},{... | collective-permute-start | bytes 3145736 | tf_op jit(solution)/shard_map/ppermute | solution.py:640
  1073.6 23.5 %collective-permute-start.65 = (f32[1,2048]{1,0:T(1,128)S(1)}, f32[1,2048]{1,0:T(1,128)S(1)}, u32[]{:S(2)}, u32[]{:S(2)}) collective-permute-start(f32[1,2048]{1,0:T(1,128)S(1)} %add.343), channel_id=1, source_target_pairs={{0,16},{8,24},{16,0},{24,8},{1,17},{9,25},{17,1},{25,9},{2,18},{10... | collective-permute-start | bytes 24584 | tf_op jit(solution)/shard_map/ppermute | solution.py:539
  1078.4 39.8 %collective-permute-start.81 = (bf16[2048,256]{1,0:T(8,128)(2,1)}, bf16[2048,256]{1,0:T(8,128)(2,1)}, u32[]{:S(2)}, u32[]{:S(2)}) collective-permute-start(bf16[2048,256]{1,0:T(8,128)(2,1)} %add_convert_fusion.7), channel_id=1, source_target_pairs={{8,16},{16,8},{9,17},{17,9},{10,18},{18,10},{11,19},{19,11},{12,20... | collective-permute-start | bytes 3145736 | tf_op jit(solution)/shard_map/ppermute | solution.py:637
  1097.7 39.0 %collective-permute-start.76 = (bf16[2048,256]{1,0:T(8,128)(2,1)S(1)}, bf16[2048,256]{1,0:T(8,128)(2,1)S(1)}, u32[]{:S(2)}, u32[]{:S(2)}) collective-permute-start(bf16[2048,256]{1,0:T(8,128)(2,1)S(1)} %copy-done.9), channel_id=1, source_target_pairs={{8,0},{16,24},{9,1},{17,25},{10,2},{18,26},{11,3},{19,27},{12,4},{... | collective-permute-start | bytes 3145736 | tf_op jit(solution)/shard_map/ppermute | solution.py:640
  1117.0 42.1 %collective-permute-start.79 = (bf16[2048,256]{1,0:T(8,128)(2,1)S(1)}, bf16[2048,256]{1,0:T(8,128)(2,1)S(1)}, u32[]{:S(2)}, u32[]{:S(2)}) collective-permute-start(bf16[2048,256]{1,0:T(8,128)(2,1)S(1)} %copy-done.10), channel_id=1, source_target_pairs={{8,0},{16,24},{9,1},{17,25},{10,2},{18,26},{11,3},{19,27},{12,4},{... | collective-permute-start | bytes 3145736 | tf_op jit(solution)/shard_map/ppermute | solution.py:640
  1120.1 61.5 %collective-permute-start.82 = (bf16[2048,256]{1,0:T(8,128)(2,1)S(1)}, bf16[2048,256]{1,0:T(8,128)(2,1)}, u32[]{:S(2)}, u32[]{:S(2)}) collective-permute-start(bf16[2048,256]{1,0:T(8,128)(2,1)S(1)} %add_convert_fusion.6), channel_id=1, source_target_pairs={{8,0},{16,24},{9,1},{17,25},{10,2},{18,26},{11,3},{19,27},{12,4},{... | collective-permute-start | bytes 3145736 | tf_op jit(solution)/shard_map/ppermute | solution.py:640
  (82 other events, 1456.5 us)
Sparse Core Ops, SparseCore 0:
  20.9 95.9 all-gather.6
  119.4 138.7 all-gather.4
  261.5 51.3 reduce-scatter.5
  373.3 67.7 reduce-scatter.11
  445.0 59.0 reduce-scatter.13
  558.4 97.0 reduce-scatter.7
  897.4 85.4 reduce-scatter.9
